TPU v7x, 32 devices: a whole 2x2x4 slice. The times are simulated.
32 devices in a mesh: dp: 16 (over z, y, core), section: 2 (over x).
Axes of the slice: x: 2, y: 2, z: 4, core: 2. Of those that a mesh axis runs over, the one named last changes fastest.
Arguments:
- patches: bfloat16 [48, 196, 768], P('dp'), may hold values from -6 to 6
- block_mask: int32 [48, 196], P('dp'), may hold values 0 or 1
- mask_token: bfloat16 [768], replicated, may hold values from -6 to 6
- norm_gains: float32 [2, 2, 768], P('section'), may hold values from 0.1 to 1.9
- norm_shifts: float32 [2, 2, 768], P('section'), may hold values from -2 to 2
- w_qkv: bfloat16 [2, 768, 2304], P('section'), may hold values from -0.21875 to 0.21875
- qv_bias: float32 [2, 2, 768], P('section'), may hold values from -3 to 3
- w_out: bfloat16 [2, 768, 768], P('section'), may hold values from -0.875 to 0.875
- out_bias: float32 [2, 768], P('section'), may hold values from -3 to 3
- w_up: bfloat16 [2, 768, 3072], P('section'), may hold values from -0.21875 to 0.21875
- up_bias: float32 [2, 3072], P('section'), may hold values from -3 to 3
- w_down: bfloat16 [2, 3072, 768], P('section'), may hold values from -0.15625 to 0.15625
- down_bias: float32 [2, 768], P('section'), may hold values from -3 to 3
- cotangent: bfloat16 [48, 196, 768], P('dp'), may hold values from -6 to 6
Outputs:
- boundary: float32 [2, 48, 196, 768], P('section', 'dp')
- token_grad: float32 [768], replicated
- gains_grad: float32 [2, 2, 768], P('section', None, 'dp')
- shifts_grad: float32 [2, 2, 768], P('section', None, 'dp')
- qkv_grad: float32 [2, 768, 2304], P('section', None, 'dp')
- qv_bias_grad: float32 [2, 2, 768], P('section', None, 'dp')
- out_grad: float32 [2, 768, 768], P('section', None, 'dp')
- out_bias_grad: float32 [2, 768], P('section', 'dp')
- up_grad: float32 [2, 768, 3072], P('section', None, 'dp')
- up_bias_grad: float32 [2, 3072], P('section', 'dp')
- down_grad: float32 [2, 3072, 768], P('section', None, 'dp')
- down_bias_grad: float32 [2, 768], P('section', 'dp')
All inputs are finite; a program needn't handle non-finite values. No bound on the sum of `block_mask` on one device may be relied on, other than what follows from the above.
Results may differ from a plain program's by a relative error of at most 0.015.
Values may be sent and summed in bfloat16 or wider, within the bound.
A program may use at most 256 MiB of HBM per device.

v0:
```python
import math

import jax
import jax.numpy as jnp
from jax import lax
from jax.sharding import PartitionSpec as P

HEADS = 12
MICRO = 3


EPS = 1e-06
NARROW = jnp.bfloat16
WIDE = jnp.float32


def from_behind(x, axis, by):
    length = lax.axis_size(axis)
    pairs = [(i, i + by) for i in range(length) if 0 <= i + by < length]
    return lax.ppermute(x, axis, pairs)


def normalize(values, gain, shift):
    centered = values - jnp.mean(values, axis=-1, keepdims=True)
    variance = jnp.mean(centered * centered, axis=-1, keepdims=True)
    return centered * lax.rsqrt(variance + EPS) * gain + shift


def gelu_exact(values):
    return jax.nn.gelu(values, approximate=False)


def split_heads(triple, width_all):
    batch_size, length = (triple.shape[0], triple.shape[1])
    shape_heads = (batch_size, length, HEADS, width_all // HEADS)
    queries = triple[..., :width_all].reshape(shape_heads)
    key_rows = triple[..., width_all : 2 * width_all].reshape(shape_heads)
    value_rows = triple[..., 2 * width_all :].reshape(shape_heads)
    return (queries, key_rows, value_rows)


def layer_forward(entry_rows, weights):
    norm_gains, norm_shifts, w_qkv, qv_bias, w_out, out_bias, w_up, up_bias, w_down, down_bias = (
        weights
    )
    batch_size, length, width_all = entry_rows.shape
    score_scale = 1.0 / math.sqrt(width_all // HEADS)
    first_in = normalize(entry_rows, norm_gains[0], norm_shifts[0]).astype(NARROW)
    joined = jnp.concatenate([qv_bias[0], jnp.zeros_like(qv_bias[0]), qv_bias[1]])
    triple = (
        jnp.einsum("bsd,de->bse", first_in, w_qkv, preferred_element_type=WIDE) + joined
    ).astype(NARROW)
    queries, key_rows, value_rows = split_heads(triple, width_all)
    scores = (
        jnp.einsum("bqhd,bkhd->bhqk", queries, key_rows, preferred_element_type=WIDE) * score_scale
    )
    row_peak = jnp.max(scores, axis=-1, keepdims=True)
    log_total = row_peak + jnp.log(jnp.sum(jnp.exp(scores - row_peak), axis=-1, keepdims=True))
    attention = jnp.exp(scores - log_total).astype(NARROW)
    mixture = jnp.einsum("bhqk,bkhd->bqhd", attention, value_rows, preferred_element_type=WIDE)
    mixture = mixture.reshape(batch_size, length, width_all).astype(NARROW)
    middle = (
        entry_rows
        + jnp.einsum("bsd,de->bse", mixture, w_out, preferred_element_type=WIDE)
        + out_bias
    )
    second_in = normalize(middle, norm_gains[1], norm_shifts[1]).astype(NARROW)
    hidden = jnp.einsum("bsd,df->bsf", second_in, w_up, preferred_element_type=WIDE) + up_bias
    active = gelu_exact(hidden).astype(NARROW)
    result = (
        middle + jnp.einsum("bsf,fd->bsd", active, w_down, preferred_element_type=WIDE) + down_bias
    )
    return (
        result,
        (entry_rows, first_in, triple, log_total, mixture, middle, second_in, hidden, active),
    )


def vacant_forward(entry_rows, hidden_width):
    batch_size, length, width_all = entry_rows.shape
    plain = jnp.zeros((batch_size, length, width_all), WIDE)
    narrow = jnp.zeros((batch_size, length, width_all), NARROW)
    stored = (
        plain,
        narrow,
        jnp.zeros((batch_size, length, 3 * width_all), NARROW),
        jnp.zeros((batch_size, HEADS, length, 1), WIDE),
        narrow,
        plain,
        narrow,
        jnp.zeros((batch_size, length, hidden_width), WIDE),
        jnp.zeros((batch_size, length, hidden_width), NARROW),
    )
    return (plain, stored)


def mlp_vacant(stored):
    return (
        jnp.zeros_like(stored[8]),
        jnp.zeros(stored[5].shape, NARROW),
        jnp.zeros_like(stored[6]),
        jnp.zeros(stored[7].shape, NARROW),
    )


def attention_vacant(stored):
    return (
        jnp.zeros_like(stored[4]),
        jnp.zeros(stored[5].shape, NARROW),
        jnp.zeros_like(stored[1]),
        jnp.zeros_like(stored[2]),
    )


def mlp_backward(incoming, stored, weights):
    entry_rows, first_in, triple, log_total, mixture, middle, second_in, hidden, active = stored
    norm_gains, norm_shifts, w_qkv, qv_bias, w_out, out_bias, w_up, up_bias, w_down, down_bias = (
        weights
    )
    out_low = incoming.astype(NARROW)
    down_bias_part = jnp.sum(incoming, axis=(0, 1))
    back_active = jnp.einsum("bsd,fd->bsf", out_low, w_down, preferred_element_type=WIDE)
    back_hidden = jax.vjp(gelu_exact, hidden)[1](back_active)[0]
    up_bias_part = jnp.sum(back_hidden, axis=(0, 1))
    hidden_low = back_hidden.astype(NARROW)
    back_second = jnp.einsum("bsf,df->bsd", hidden_low, w_up, preferred_element_type=WIDE)
    back_middle, back_gain, back_shift = jax.vjp(normalize, middle, norm_gains[1], norm_shifts[1])[
        1
    ](back_second)
    small = (back_gain, back_shift, up_bias_part, down_bias_part)
    return (small, back_middle + incoming, (active, out_low, second_in, hidden_low))


def attention_backward(back_middle, stored, weights):
    entry_rows, first_in, triple, log_total, mixture, middle, second_in, hidden, active = stored
    norm_gains, norm_shifts, w_qkv, qv_bias, w_out, out_bias, w_up, up_bias, w_down, down_bias = (
        weights
    )
    batch_size, length, width_all = back_middle.shape
    score_scale = 1.0 / math.sqrt(width_all // HEADS)
    middle_low = back_middle.astype(NARROW)
    out_bias_part = jnp.sum(back_middle, axis=(0, 1))
    back_mixture = jnp.einsum("bse,de->bsd", middle_low, w_out, preferred_element_type=WIDE).astype(
        NARROW
    )
    back_heads = back_mixture.reshape(batch_size, length, HEADS, width_all // HEADS)
    queries, key_rows, value_rows = split_heads(triple, width_all)
    scores = (
        jnp.einsum("bqhd,bkhd->bhqk", queries, key_rows, preferred_element_type=WIDE) * score_scale
    )
    attention = jnp.exp(scores - log_total)
    attention_low = attention.astype(NARROW)
    back_values = jnp.einsum(
        "bhqk,bqhd->bkhd", attention_low, back_heads, preferred_element_type=WIDE
    )
    back_weights = jnp.einsum(
        "bqhd,bkhd->bhqk", back_heads, value_rows, preferred_element_type=WIDE
    )
    back_scores = attention * (
        back_weights - jnp.sum(attention * back_weights, axis=-1, keepdims=True)
    )
    back_scores = back_scores.astype(NARROW)
    back_queries = (
        jnp.einsum("bhqk,bkhd->bqhd", back_scores, key_rows, preferred_element_type=WIDE)
        * score_scale
    )
    back_keys = (
        jnp.einsum("bhqk,bqhd->bkhd", back_scores, queries, preferred_element_type=WIDE)
        * score_scale
    )
    flat_shape = (batch_size, length, width_all)
    query_flat = back_queries.reshape(flat_shape)
    value_flat = back_values.reshape(flat_shape)
    back_triple = jnp.concatenate([query_flat, back_keys.reshape(flat_shape), value_flat], axis=-1)
    bias_part = jnp.stack([jnp.sum(query_flat, axis=(0, 1)), jnp.sum(value_flat, axis=(0, 1))])
    triple_low = back_triple.astype(NARROW)
    back_first = jnp.einsum("bse,de->bsd", triple_low, w_qkv, preferred_element_type=WIDE)
    back_entry, back_gain, back_shift = jax.vjp(
        normalize, entry_rows, norm_gains[0], norm_shifts[0]
    )[1](back_first)
    small = (back_gain, back_shift, bias_part, out_bias_part)
    return (small, back_entry + back_middle, (mixture, middle_low, first_in, triple_low))


def add_small(totals, mlp_small, attention_small):
    parts = list(totals)
    parts[0] = parts[0] + jnp.stack([attention_small[0], mlp_small[0]])
    parts[1] = parts[1] + jnp.stack([attention_small[1], mlp_small[1]])
    parts[3] = parts[3] + attention_small[2]
    parts[5] = parts[5] + attention_small[3]
    parts[7] = parts[7] + mlp_small[2]
    parts[9] = parts[9] + mlp_small[3]
    return tuple(parts)


def mlp_weights(kept, totals):
    active, out_low, second_in, hidden_low = kept
    parts = list(totals)
    parts[8] = parts[8] + jnp.einsum("bsf,bsd->fd", active, out_low, preferred_element_type=WIDE)
    parts[6] = parts[6] + jnp.einsum(
        "bsd,bsf->df", second_in, hidden_low, preferred_element_type=WIDE
    )
    return tuple(parts)


def attention_weights(kept, totals):
    mixture, middle_low, first_in, triple_low = kept
    parts = list(totals)
    parts[4] = parts[4] + jnp.einsum(
        "bsd,bse->de", mixture, middle_low, preferred_element_type=WIDE
    )
    parts[2] = parts[2] + jnp.einsum(
        "bsd,bse->de", first_in, triple_low, preferred_element_type=WIDE
    )
    return tuple(parts)


def on_device(
    patches,
    block_mask,
    mask_token,
    norm_gains,
    norm_shifts,
    w_qkv,
    qv_bias,
    w_out,
    out_bias,
    w_up,
    up_bias,
    w_down,
    down_bias,
    cotangent,
):
    section_index = lax.axis_index("section")
    leading = section_index == 0
    image_count, length, width_all = patches.shape
    per_batch = image_count // MICRO
    hidden_width = w_up.shape[2]
    weights = (
        norm_gains[0],
        norm_shifts[0],
        w_qkv[0],
        qv_bias[0],
        w_out[0],
        out_bias[0],
        w_up[0],
        up_bias[0],
        w_down[0],
        down_bias[0],
    )
    covered = (block_mask == 1)[..., None]
    inputs = jnp.where(covered, mask_token.astype(WIDE), patches.astype(WIDE))

    def forward_branch(entry_rows):
        return layer_forward(entry_rows, weights)

    def vacant_branch(entry_rows):
        return vacant_forward(entry_rows, hidden_width)

    stored_turns = []
    finals = []
    outgoing = None
    for turn_index in range(MICRO + 1):
        own_batch = min(turn_index, MICRO - 1)
        own_rows = inputs[own_batch * per_batch : (own_batch + 1) * per_batch]
        if turn_index == 0:
            entry_rows = own_rows
        else:
            arrived = from_behind(outgoing, "section", 1)
            if turn_index == MICRO:
                entry_rows = arrived.astype(WIDE)
            else:
                entry_rows = jnp.where(leading, own_rows, arrived.astype(WIDE))
        working = jnp.where(leading, turn_index < MICRO, turn_index >= 1)
        result, stored = lax.cond(working, forward_branch, vacant_branch, entry_rows)
        stored_turns.append(stored)
        if turn_index >= 1:
            finals.append(result)
        outgoing = result.astype(NARROW)
    totals = tuple((jnp.zeros(item.shape, WIDE) for item in weights))
    back_rows = []
    token_part = jnp.zeros((width_all,), WIDE)
    sending = None
    pending_mlp = mlp_vacant(stored_turns[0])
    pending_attention = attention_vacant(stored_turns[0])
    mlp_zeros = (
        jnp.zeros((width_all,), WIDE),
        jnp.zeros((width_all,), WIDE),
        jnp.zeros((hidden_width,), WIDE),
        jnp.zeros((width_all,), WIDE),
    )
    attention_zeros = (
        jnp.zeros((width_all,), WIDE),
        jnp.zeros((width_all,), WIDE),
        jnp.zeros((2, width_all), WIDE),
        jnp.zeros((width_all,), WIDE),
    )
    for turn_index in range(MICRO + 1):
        own_batch = min(turn_index, MICRO - 1)
        own_rows = cotangent[own_batch * per_batch : (own_batch + 1) * per_batch].astype(WIDE)
        if turn_index == 0:
            incoming = own_rows
        else:
            arrived = from_behind(sending, "section", -1)
            if turn_index == MICRO:
                incoming = arrived.astype(WIDE)
            else:
                incoming = jnp.where(leading, arrived.astype(WIDE), own_rows)
        if turn_index == 0:
            stored = stored_turns[1]
        elif turn_index == MICRO:
            stored = stored_turns[MICRO - 1]
        else:
            stored = jax.tree.map(
                lambda lower, upper: jnp.where(leading, lower, upper),
                stored_turns[turn_index - 1],
                stored_turns[turn_index + 1],
            )
        working = jnp.where(leading, turn_index >= 1, turn_index < MICRO)

        def mlp_branch(operand, stored=stored):
            return mlp_backward(operand, stored, weights)

        def mlp_skip(operand, stored=stored):
            return (mlp_zeros, jnp.zeros_like(operand), mlp_vacant(stored))

        def attention_branch(operand, stored=stored):
            return attention_backward(operand, stored, weights)

        def attention_skip(operand, stored=stored):
            return (attention_zeros, jnp.zeros_like(operand), attention_vacant(stored))

        mlp_small, back_middle, mlp_kept = lax.cond(working, mlp_branch, mlp_skip, incoming)
        attention_small, back_entry, attention_kept = lax.cond(
            working, attention_branch, attention_skip, back_middle
        )
        sending = back_entry.astype(NARROW)
        totals = add_small(totals, mlp_small, attention_small)
        totals = attention_weights(pending_attention, mlp_weights(pending_mlp, totals))
        pending_mlp, pending_attention = (mlp_kept, attention_kept)
        if turn_index >= 1:
            back_rows.append(back_entry)
            batch_covered = covered[(turn_index - 1) * per_batch : turn_index * per_batch]
            token_part = token_part + jnp.sum(
                jnp.where(batch_covered, back_entry, 0.0), axis=(0, 1)
            )
    totals = attention_weights(pending_attention, mlp_weights(pending_mlp, totals))
    summed = (
        lax.psum_scatter(totals[0][None], "dp", scatter_dimension=2, tiled=True),
        lax.psum_scatter(totals[1][None], "dp", scatter_dimension=2, tiled=True),
        lax.psum_scatter(totals[2][None], "dp", scatter_dimension=2, tiled=True),
        lax.psum_scatter(totals[3][None], "dp", scatter_dimension=2, tiled=True),
        lax.psum_scatter(totals[4][None], "dp", scatter_dimension=2, tiled=True),
        lax.psum_scatter(totals[5][None], "dp", scatter_dimension=1, tiled=True),
        lax.psum_scatter(totals[6][None], "dp", scatter_dimension=2, tiled=True),
        lax.psum_scatter(totals[7][None], "dp", scatter_dimension=1, tiled=True),
        lax.psum_scatter(totals[8][None], "dp", scatter_dimension=2, tiled=True),
        lax.psum_scatter(totals[9][None], "dp", scatter_dimension=1, tiled=True),
    )
    grad_scale = 1.0 / math.sqrt(image_count * lax.axis_size("dp") * length)
    token_term = jnp.where(leading, token_part, 0.0)
    token_total = lax.psum(token_term, ("dp", "section"))
    gradient_rows = jnp.concatenate(back_rows, axis=0)
    final_rows = jnp.concatenate(finals, axis=0)
    boundary = jnp.where(leading, jnp.where(covered, 0.0, gradient_rows), final_rows)[None]
    return (
        boundary,
        token_total * grad_scale,
        summed[0] * grad_scale,
        summed[1] * grad_scale,
        summed[2] * grad_scale,
        summed[3] * grad_scale,
        summed[4] * grad_scale,
        summed[5] * grad_scale,
        summed[6] * grad_scale,
        summed[7] * grad_scale,
        summed[8] * grad_scale,
        summed[9] * grad_scale,
    )


def solution(mesh):
    return jax.shard_map(
        on_device,
        mesh=mesh,
        in_specs=(
            P("dp", None, None),
            P("dp", None),
            P(),
            P("section", None, None),
            P("section", None, None),
            P("section", None, None),
            P("section", None, None),
            P("section", None, None),
            P("section", None),
            P("section", None, None),
            P("section", None),
            P("section", None, None),
            P("section", None),
            P("dp", None, None),
        ),
        out_specs=(
            P("section", "dp", None, None),
            P(),
            P("section", None, "dp"),
            P("section", None, "dp"),
            P("section", None, "dp"),
            P("section", None, "dp"),
            P("section", None, "dp"),
            P("section", "dp"),
            P("section", None, "dp"),
            P("section", "dp"),
            P("section", None, "dp"),
            P("section", "dp"),
        ),
        check_vma=False,
    )
```

profile of v0, /device:TPU:0, one launch (start us, length us, event | category | flops | bytes accessed | tf_op | source)
XLA Modules:
  0.0 1308.0 jit_solution(4337229210860589672)
XLA Ops:
  11.5 30.3 %conditional.6 = (f32[1,196,768]{2,1,0:T(8,128)S(1)}, f32[1,196,768]{2,1,0:T(8,128)S(1)}, bf16[1,196,768]{2,1,0:T(8,128)(2,1)}, bf16[1,196,2304]{2,1,0:T(8,128)(...) conditional(s32[]{:T(128)} %convert_element_type.401, ...), branch_computations={%region_0.1_spmd, %region_1.8_spmd} | conditional | flops 2940341248 | bytes 61253780 | solution.py:275
  28.5 8.3 fusion.4
  127.8 21.3 %collective-permute-done.2 = bf16[1,196,768]{2,1,0:T(8,128)(2,1)} collective-permute-done((bf16[1,196,768]{2,1,0:T(8,128)(2,1)}, bf16[1,196,768]{2,1,0:T(8,128)(2,1)}, u32[]{:S(2)}, u32[]{:S(2)}) %collective-permute-start.2) | collective-permute-done | bytes 301088 | tf_op jit(solution)/shard_map/ppermute | solution.py:20
  149.1 9.0 fusion.318
  197.1 25.9 %collective-permute-start.3 = (bf16[1,196,768]{2,1,0:T(8,128)(2,1)}, bf16[1,196,768]{2,1,0:T(8,128)(2,1)}, u32[]{:S(2)}, u32[]{:S(2)}) collective-permute-start(bf16[1,196,768]{2,1,0:T(8,128)(2,1)} %get-tuple-element.768), channel_id=1, source_target_pairs={{0,1},{2,3},{4,5},{6,7},{8,9},{10,11},{12,13},{14,15},{16,17},{18,... | collective-permute-start | bytes 903176 | tf_op jit(solution)/shard_map/ppermute | solution.py:20
  237.0 9.3 conditional.9
  247.5 9.8 fusion.317
  300.5 30.0 %collective-permute-done.5 = bf16[1,196,768]{2,1,0:T(8,128)(2,1)} collective-permute-done((bf16[1,196,768]{2,1,0:T(8,128)(2,1)}, bf16[1,196,768]{2,1,0:T(8,128)(2,1)}, u32[]{:S(2)}, u32[]{:S(2)}) %collective-permute-start.5) | collective-permute-done | bytes 301088 | tf_op jit(solution)/shard_map/ppermute | solution.py:20
  331.6 21.8 %conditional.10 = (f32[3072]{0:T(1024)S(1)}, f32[768]{0:T(1024)S(1)}, f32[1,196,768]{2,1,0:T(8,128)}, f32[1,1,768]{2,1,0:T(1,128)S(1)}, f32[1,1,768]{2,1,0:T(1,1...) conditional(s32[]{:T(128)} %convert_element_type.401, ...), branch_computations={%region_68.69_spmd, %region_69.78_spmd} | conditional | flops 1897100288 | bytes 32379312 | solution.py:333
  332.3 9.6 convert_bitcast_fusion.3
  354.5 24.2 %conditional.11 = (f32[2,768]{1,0:T(2,128)S(1)}, f32[768]{0:T(1024)S(1)}, f32[1,196,768]{2,1,0:T(8,128)}, f32[1,1,768]{2,1,0:T(1,128)}, f32[1,1,768]{2,1,0:T(1,1...) conditional(s32[]{:T(128)} %convert_element_type.401, ...), branch_computations={%region_78.79_spmd, %region_79.90_spmd} | conditional | flops 1230939392 | bytes 84293544 | solution.py:334
  387.7 14.5 %add_bitcast_fusion.2 = f32[1,768,2304]{2,1,0:T(8,128)} fusion(f32[768,2304]{1,0:T(8,128)} %fusion.184, f32[768,2304]{1,0:T(8,128)} %fusion.186, f32[768,2304]{1,0:T(8,128)} %fusion.188, f32[768,2304]{1,0:T(8,128)} %fusion.323, bf16[196,768]{1,0:T(8,128)(2,1)S(1)} %copy-done.42, bf16[196,2304]{0,1:T(8,128)(2,1)S(1)} %copy-done.44), kind=kOutput, calls=%fused_computation.235 | convolution fusion | flops 700710912 | bytes 36593664 | tf_op jit(solution)/shard_map/bsd,bse->de/dot_general | solution.py:212
  403.8 16.6 %copy.183 = f32[1,768,2304]{1,0,2:T(1,128)} copy(f32[1,768,2304]{2,1,0:T(8,128)} %add_bitcast_fusion.2) | data formatting | bytes 14155776 | tf_op jit(solution)/shard_map/broadcast_in_dim | solution.py:351
  448.2 17.6 %add_bitcast_fusion.1 = f32[1,768,3072]{2,1,0:T(8,128)} fusion(f32[768,3072]{1,0:T(8,128)} %fusion.138, f32[768,3072]{1,0:T(8,128)} %fusion.142, f32[768,3072]{1,0:T(8,128)} %fusion.174, f32[768,3072]{1,0:T(8,128)} %fusion.325, bf16[196,768]{1,0:T(8,128)(2,1)S(1)} %copy-done.89, bf16[196,3072]{1,0:T(8,128)(2,1)} %get-tuple-element.422), kind=kOutput, calls=%fused_computation.234 | convolution fusion | flops 934281216 | bytes 48691200 | tf_op jit(solution)/shard_map/bsd,bsf->df/dot_general | solution.py:200
  465.8 20.6 %copy.189 = f32[1,768,3072]{1,0,2:T(1,128)} copy(f32[1,768,3072]{2,1,0:T(8,128)} %add_bitcast_fusion.1) | data formatting | bytes 18874368 | tf_op jit(solution)/shard_map/broadcast_in_dim | solution.py:355
  511.6 17.1 %add_bitcast_fusion = f32[1,3072,768]{2,1,0:T(8,128)} fusion(f32[3072,768]{1,0:T(8,128)} %fusion.134, f32[3072,768]{1,0:T(8,128)} %fusion.136, f32[3072,768]{1,0:T(8,128)} %fusion.172, f32[3072,768]{1,0:T(8,128)} %fusion.326, bf16[196,3072]{1,0:T(8,128)(2,1)S(1)} %copy-done.39, bf16[196,768]{1,0:T(8,128)(2,1)} %get-tuple-element.430), kind=kOutput, calls=%fused_computation.233 | convolution fusion | flops 934281216 | bytes 48691200 | tf_op jit(solution)/shard_map/bsf,bsd->fd/dot_general | solution.py:199
  528.7 20.8 %copy.190 = f32[1,3072,768]{1,0,2:T(1,128)} copy(f32[1,3072,768]{2,1,0:T(8,128)} %add_bitcast_fusion) | data formatting | bytes 18874368 | tf_op jit(solution)/shard_map/broadcast_in_dim | solution.py:357
  558.6 40.0 %psum.7 = f32[768]{0:T(1024)S(1)} all-reduce(f32[768]{0:T(1024)S(1)} %add_select_fusion), channel_id=1, replica_groups=mesh['dp'=16,'section'=2] {'dp','section'}, use_global_device_ids=true, to_apply=%region_93.94 | all-reduce | flops 768 | bytes 6144 | tf_op jit(solution)/shard_map/psum | solution.py:362
  602.6 9.7 reduce-scatter.21.cloned.1.call-done
  613.1 57.8 %reduce-scatter.23.cloned.1.call-done = f32[48,2]{1,0:T(8,128)} async-done(((f32[768,2]{1,0:T(8,128)}), f32[48,2]{1,0:T(8,128)}) %reduce-scatter.23.cloned.1.call-update) | async-done | bytes 400
  673.3 60.0 %reduce-scatter.27.cloned.1.call-done = f32[192,1]{1,0:T(8,128)} async-done(((f32[3072,1]{1,0:T(8,128)}), f32[192,1]{1,0:T(8,128)}) %reduce-scatter.27.cloned.1.call-update) | async-done | bytes 784
  734.9 186.3 %all-reduce.13.cloned.1.call-done = (f32[1,768,2304]{1,0,2:T(1,128)}, f32[1,768,768]{1,0,2:T(1,128)}) async-done(((f32[1,768,2304]{1,0,2:T(1,128)}, f32[1,768,768]{1,0,2:T(1,128)}), (f32[1,768,2304]{1,0,2:T(1,128)}, f32[1,768,768]{1,0,2:T(1,128)})) %all-reduce.13.cloned.1.call-update) | async-done | bytes 9437200
  925.2 185.0 %all-reduce.9.cloned.1.call-done = f32[1,768,3072]{1,0,2:T(1,128)} async-done(((f32[1,768,3072]{1,0,2:T(1,128)}), f32[1,768,3072]{1,0,2:T(1,128)}) %all-reduce.9.cloned.1.call-update) | async-done | bytes 9437200
  1112.7 186.0 %all-reduce.11.cloned.1.call-done = f32[1,3072,768]{1,0,2:T(1,128)} async-done(((f32[1,3072,768]{1,0,2:T(1,128)}), f32[1,3072,768]{1,0,2:T(1,128)}) %all-reduce.11.cloned.1.call-update) | async-done | bytes 9437200
  (635 shorter events, 350.8 us)
Async XLA Ops:
  7.2 591.9 %reduce-scatter.25.cloned.1.call-start = ((), (), s32[]{:S(2)}) async-start(), calls=%async_computation.9 | async-start | bytes 417792
  8.8 34.8 %copy-start.111 = (pred[3,196]{1,0:T(4,128)(4,1)}, pred[3,196]{1,0:T(4,128)(4,1)S(1)}, u32[]{:S(2)}) copy-start(pred[3,196]{1,0:T(4,128)(4,1)S(1)} %broadcast_compare_fusion) | copy-start | bytes 1768
  41.8 10.2 collective-permute-start
  54.6 29.9 %copy-start.25 = (bf16[1,196,2304]{2,1,0:T(8,128)(2,1)}, bf16[1,196,2304]{2,1,0:T(8,128)(2,1)S(1)}, u32[]{:S(2)}) copy-start(bf16[1,196,2304]{2,1,0:T(8,128)(2,1)S(1)} %fusion.86) | copy-start | bytes 2709508
  76.2 24.1 %collective-permute-start.1 = (bf16[1,196,768]{2,1,0:T(8,128)(2,1)}, bf16[1,196,768]{2,1,0:T(8,128)(2,1)}, u32[]{:S(2)}, u32[]{:S(2)}) collective-permute-start(bf16[1,196,768]{2,1,0:T(8,128)(2,1)} %get-tuple-element.755), channel_id=1, source_target_pairs={{0,1},{2,3},{4,5},{6,7},{8,9},{10,11},{12,13},{14,15},{16,17},{18,... | collective-permute-start | bytes 903176 | tf_op jit(solution)/shard_map/ppermute | solution.py:20
  95.8 53.2 %collective-permute-start.2 = (bf16[1,196,768]{2,1,0:T(8,128)(2,1)}, bf16[1,196,768]{2,1,0:T(8,128)(2,1)}, u32[]{:S(2)}, u32[]{:S(2)}) collective-permute-start(bf16[1,196,768]{2,1,0:T(8,128)(2,1)} %get-tuple-element.381), channel_id=1, source_target_pairs={{1,0},{3,2},{5,4},{7,6},{9,8},{11,10},{13,12},{15,14},{17,16},{19,... | collective-permute-start | bytes 903176 | tf_op jit(solution)/shard_map/ppermute | solution.py:20
  117.3 31.7 %slice-start.2 = ((s8[4718592]{0:T(1024)(128)(4,1)}), s8[4194304]{0:T(1024)(128)(4,1)S(1)}, s32[]{:S(2)}) async-start(s8[4718592]{0:T(1024)(128)(4,1)} %bitcast.653), calls=%async_computation.17 | async-start | bytes 8388608
  127.6 30.5 %copy-start.156 = (f32[196,3072]{1,0:T(8,128)}, f32[196,3072]{1,0:T(8,128)S(1)}, u32[]{:S(2)}) copy-start(f32[196,3072]{1,0:T(8,128)S(1)} %get-tuple-element.767) | copy-start | bytes 7225348
  191.2 55.5 %collective-permute-start.4 = (bf16[1,196,768]{2,1,0:T(8,128)(2,1)}, bf16[1,196,768]{2,1,0:T(8,128)(2,1)}, u32[]{:S(2)}, u32[]{:S(2)}) collective-permute-start(bf16[1,196,768]{2,1,0:T(8,128)(2,1)} %convert_element_type.443), channel_id=1, source_target_pairs={{1,0},{3,2},{5,4},{7,6},{9,8},{11,10},{13,12},{15,14},{17,16},{19,... | collective-permute-start | bytes 903176 | tf_op jit(solution)/shard_map/ppermute | solution.py:20
  192.6 32.2 %copy-start.41 = (bf16[1,196,768]{2,1,0:T(8,128)(2,1)S(1)}, bf16[1,196,768]{2,1,0:T(8,128)(2,1)}, u32[]{:S(2)}) copy-start(bf16[1,196,768]{2,1,0:T(8,128)(2,1)} %copy-done.40) | copy-start | bytes 903172
  192.6 32.2 %copy-start.82 = (bf16[1,196,12,64]{1,3,2,0:T(8,128)(2,1)S(1)}, bf16[1,196,12,64]{1,3,2,0:T(8,128)(2,1)}, u32[]{:S(2)}) copy-start(bf16[1,196,12,64]{1,3,2,0:T(8,128)(2,1)} %get-tuple-element.747) | copy-start | bytes 903172
  192.6 32.2 %copy-start.84 = (bf16[12,64,196]{2,1,0:T(8,128)(2,1)S(1)}, bf16[12,64,196]{2,1,0:T(8,128)(2,1)}, u32[]{:S(2)}) copy-start(bf16[12,64,196]{2,1,0:T(8,128)(2,1)} %fusion.132) | copy-start | bytes 903172
  192.6 32.2 %copy-start.85 = (bf16[1,196,12,64]{1,3,2,0:T(8,128)(2,1)S(1)}, bf16[1,196,12,64]{1,3,2,0:T(8,128)(2,1)}, u32[]{:S(2)}) copy-start(bf16[1,196,12,64]{1,3,2,0:T(8,128)(2,1)} %get-tuple-element.745) | copy-start | bytes 903172
  197.1 38.0 %collective-permute-start.3 = (bf16[1,196,768]{2,1,0:T(8,128)(2,1)}, bf16[1,196,768]{2,1,0:T(8,128)(2,1)}, u32[]{:S(2)}, u32[]{:S(2)}) collective-permute-start(bf16[1,196,768]{2,1,0:T(8,128)(2,1)} %get-tuple-element.768), channel_id=1, source_target_pairs={{0,1},{2,3},{4,5},{6,7},{8,9},{10,11},{12,13},{14,15},{16,17},{18,... | collective-permute-start | bytes 903176 | tf_op jit(solution)/shard_map/ppermute | solution.py:20
  288.1 42.4 %collective-permute-start.5 = (bf16[1,196,768]{2,1,0:T(8,128)(2,1)}, bf16[1,196,768]{2,1,0:T(8,128)(2,1)}, u32[]{:S(2)}, u32[]{:S(2)}) collective-permute-start(bf16[1,196,768]{2,1,0:T(8,128)(2,1)} %convert_element_type.452), channel_id=1, source_target_pairs={{1,0},{3,2},{5,4},{7,6},{9,8},{11,10},{13,12},{15,14},{17,16},{19,... | collective-permute-start | bytes 903176 | tf_op jit(solution)/shard_map/ppermute | solution.py:20
  297.4 34.2 %copy-start.157 = (f32[196,3072]{1,0:T(8,128)S(1)}, f32[196,3072]{1,0:T(8,128)}, u32[]{:S(2)}) copy-start(f32[196,3072]{1,0:T(8,128)} %copy-done.156) | copy-start | bytes 7225348
  379.8 220.1 %reduce-scatter.29.cloned.1.call-start = ((), (), s32[]{:S(2)}) async-start(), calls=%async_computation.11 | async-start | bytes 417792
  380.9 220.9 %reduce-scatter.19.cloned.1.call-start = ((), (), s32[]{:S(2)}) async-start(), calls=%async_computation.6 | async-start | bytes 417792
  382.7 229.6 %reduce-scatter.21.cloned.1.call-start = ((), (), s32[]{:S(2)}) async-start(), calls=%async_computation.7 | async-start | bytes 417792
  384.7 286.2 %reduce-scatter.23.cloned.1.call-start = ((), (), s32[]{:S(2)}) async-start(), calls=%async_computation.8 | async-start | bytes 417792
  385.8 347.5 %reduce-scatter.27.cloned.1.call-start = ((), (), s32[]{:S(2)}) async-start(), calls=%async_computation.10 | async-start | bytes 1671168
  387.6 533.5 %all-reduce.13.cloned.1.call-start = ((), (), s32[]{:S(2)}) async-start(), calls=%async_computation.14 | async-start | bytes 18874368
  424.9 685.2 %all-reduce.9.cloned.1.call-start = ((), (), s32[]{:S(2)}) async-start(), calls=%async_computation.12 | async-start | bytes 18874368
  486.4 812.3 %all-reduce.11.cloned.1.call-start = ((), (), s32[]{:S(2)}) async-start(), calls=%async_computation.13 | async-start | bytes 18874368
  (142 other events, 821.4 us)
Sparse Core Ops, SparseCore 0:
  380.0 56.0 reduce-scatter.24
  440.0 54.5 reduce-scatter.28
  498.7 54.6 reduce-scatter.18
  557.7 54.5 reduce-scatter.20
  616.2 54.6 reduce-scatter.22
  674.8 58.4 reduce-scatter.26
  737.0 184.1 all-reduce.12
  925.3 184.8 all-reduce.8
  1113.8 184.8 all-reduce.10
where the time goes:
time: 1320 us; the launch traced here: 1310 us
  waiting for transfers between devices  736 us (56%)
  matrix products  248 us (19%)
  local copies, waits for them, and re-layouts  159 us (12%)
  other arithmetic  69.5 us (5%)
  blocking collectives  40 us (3%)
  starting transfers between devices  36.4 us (3%)
  between operations  17.8 us (1%)
    unnamed x18, waiting for transfers between devices  685 us
    ppermute x6, waiting for transfers between devices, from_behind(): return lax.ppermute(x, axis, pairs)  51.3 us
    dot_general x5, matrix products, mlp_weights(): jnp.einsum('bsf,bsd->fd', active, out_low, preferred_element_type=WIDE)  41.7 us
    dot_general x5, matrix products, mlp_weights(): jnp.einsum('bsd,bsf->df', second_in, hidden_low, preferred_element_type=W...  40.6 us
    psum x1, blocking collectives, on_device(): token_total = lax.psum(token_term, ('dp', 'section'))  40 us
    ppermute x6, starting transfers between devices, from_behind(): return lax.ppermute(x, axis, pairs)  35.3 us
    dot_general x5, matrix products, attention_weights(): jnp.einsum('bsd,bse->de', first_in, triple_low, preferred_element_type=WIDE)  33.1 us
    dot_general x3, matrix products, mlp_backward(): jnp.einsum('bsd,fd->bsf', out_low, w_down, preferred_element_type=WIDE)  28.5 us
  transfers between devices with their start and end apart: 15, of which 8 were waited for; matrix products, arithmetic and copies ran while one was open for 21% of the time, Pallas kernels for 0%

commit v1 on v0

v1 whole, which is shorter than its diff:
```python
import functools
import math

import jax
import jax.numpy as jnp
from jax import lax
from jax.experimental import pallas as pl
from jax.experimental.pallas import tpu as pltpu
from jax.sharding import PartitionSpec as P

HEADS = 12
EPS = 1e-06
BF = jnp.bfloat16
F32 = jnp.float32
HALVINGS = (1, 2, 8, 4)
UNITS = 12
UP, OUT, QKV, DOWN_W = 4, 8, 9, 12
SMALL = 16
INV_SQRT2 = 1.0 / math.sqrt(2.0)
INV_SQRT2PI = 1.0 / math.sqrt(2.0 * math.pi)


def dot(a, b, contract_a, contract_b):
    return lax.dot_general(
        a, b, (((contract_a,), (contract_b,)), ((), ())), preferred_element_type=F32
    )


def fold8(x):
    rows, width = x.shape
    return jnp.sum(x.reshape(rows // 8, 8, width), axis=0)


def kernel(geo, *refs):
    (n, images, seq, pad, width, scale) = geo
    reduce_here = n == 16
    total_rows = images * pad
    block = width // 16
    names = ["patches", "cotangent", "mask", "token", "gains", "shifts", "qv_bias", "out_bias", "up_bias"]
    names += ["down_bias", "w_qkv", "w_out", "w_up", "w_down", "bound", "grads", "small", "wg", "x", "n1"]
    names += ["a1", "qkv", "o", "n2", "a2", "act", "gp", "dy", "send", "prob", "rstd", "mcol", "yb", "da"]
    names += ["tb", "do", "pin", "sm", "sms", "smr", "pin_sem", "w_sem", "out_sem", "fs", "fr", "bs", "br"]
    if reduce_here:
        names += ["rc", "ry", "rz", "rw", "cs", "cr", "ys", "yr", "zs", "zr", "ws", "wr", "ss", "sr"]
    r = dict(zip(names, refs, strict=True))
    wg = r["wg"]
    me = lax.axis_index("dp")
    sec = lax.axis_index("section")
    first, second = sec == 0, sec == 1

    def dp_at(bit):
        mine = lax.rem(me // bit, 2)
        return {"dp": me + bit - 2 * bit * mine, "section": sec}

    across = {"dp": me, "section": 1 - sec}
    partners = [across] + ([dp_at(bit) for bit in HALVINGS] if reduce_here else [])

    def unit_rows(unit, offset=0, size=width):
        return pl.ds(pl.multiple_of(unit * width + offset, 16), size)

    weight_copies = []
    for j in range(3):
        weight_copies.append((QKV + j, r["w_qkv"].at[0, :, pl.ds(width * j, width)]))
    weight_copies.append((OUT, r["w_out"].at[0]))
    for j in range(4):
        weight_copies.append((UP + j, r["w_up"].at[0, :, pl.ds(width * j, width)]))
    for j in range(4):
        weight_copies.append((DOWN_W + j, r["w_down"].at[0, pl.ds(width * j, width), :]))

    def weight_copy(index):
        unit, source = weight_copies[index]
        return pltpu.make_async_copy(source, wg.at[unit_rows(unit), :], r["w_sem"].at[index])

    @pl.when(first)
    def _():
        pltpu.make_async_copy(r["patches"], r["pin"], r["pin_sem"]).start()

    @pl.when(second)
    def _():
        pltpu.make_async_copy(r["cotangent"], r["pin"], r["pin_sem"]).start()

    for index in range(UNITS):
        weight_copy(index).start()

    barrier = pltpu.get_barrier_semaphore()
    for partner in partners:
        pl.semaphore_signal(barrier, inc=1, device_id=partner)
    pl.semaphore_wait(barrier, len(partners))

    r["sm"][...] = jnp.zeros_like(r["sm"])
    pltpu.make_async_copy(r["patches"], r["pin"], r["pin_sem"]).wait()

    def image_rows(img, offset=0, size=pad):
        return pl.ds(pl.multiple_of(img * pad + offset, 16), size)

    def forward_send(img):
        rows = image_rows(img)
        return pltpu.make_async_remote_copy(
            src_ref=r["send"].at[rows, :],
            dst_ref=r["x"].at[rows, :],
            send_sem=r["fs"].at[img],
            recv_sem=r["fr"].at[img],
            device_id=across,
        )

    def backward_send(img):
        rows = image_rows(img)
        return pltpu.make_async_remote_copy(
            src_ref=r["send"].at[rows, :],
            dst_ref=r["dy"].at[rows, :],
            send_sem=r["bs"].at[img],
            recv_sem=r["br"].at[img],
            device_id=across,
        )

    def bound_copy(img):
        rows = image_rows(img)
        return pltpu.make_async_copy(
            r["yb"].at[rows, :], r["bound"].at[img], r["out_sem"].at[img]
        )

    def row_blocks(img):
        return [image_rows(img, 16 * b, 16) for b in range(pad // 16)]

    def norm_forward(img, source, which, normed, scaled):
        gain = r["gains"][which : which + 1, :]
        shift = r["shifts"][which : which + 1, :]
        for rows in row_blocks(img):
            values = source[rows, :].astype(F32)
            centered = values - jnp.mean(values, axis=1, keepdims=True)
            variance = jnp.mean(centered * centered, axis=1, keepdims=True)
            inverse = lax.rsqrt(variance + EPS)
            unit = centered * inverse
            r["rstd"][which, rows, :] = inverse
            normed[rows, :] = unit.astype(BF)
            scaled[rows, :] = (unit * gain + shift).astype(BF)

    def halves(values):
        lane = lax.broadcasted_iota(jnp.int32, values.shape, 1)
        zero = jnp.zeros_like(values)
        low = lane < width // HEADS
        return jnp.where(low, values, zero), jnp.where(low, zero, values)

    def attention_forward(img, pair):
        rows = image_rows(img)
        lanes = pl.ds(pl.multiple_of(128 * pair, 128), 128)
        queries = r["qkv"][0, rows, lanes]
        keys = r["qkv"][1, rows, lanes]
        values = r["qkv"][2, rows, lanes]
        mixed = []
        for head, part in enumerate(halves(queries)):
            scores = dot(keys, part, 1, 1)
            key_at = lax.broadcasted_iota(jnp.int32, scores.shape, 0)
            scores = jnp.where(key_at < seq, scores, -1e30)
            raised = jnp.exp(scores - jnp.max(scores, axis=0, keepdims=True))
            share = 1.0 / jnp.sum(raised, axis=0, keepdims=True)
            prob = (raised * share).astype(BF)
            r["prob"][img * HEADS + 2 * pair + head] = prob
            mixed.append(dot(prob, values, 0, 0))
        lane = lax.broadcasted_iota(jnp.int32, mixed[0].shape, 1)
        r["o"][rows, lanes] = jnp.where(lane < width // HEADS, mixed[0], mixed[1]).astype(BF)

    def wait_weights(step, indices):
        @pl.when(step == 0)
        def _():
            for index in indices:
                weight_copy(index).wait()

    def forward(step, img):
        rows = image_rows(img)

        @pl.when(first)
        def _():
            tail = image_rows(img, seq // 16 * 16, 16)
            r["x"][tail, :] = jnp.zeros((16, width), BF)
            row = r["mask"][pl.ds(img, 1), :]
            at_row = lax.broadcasted_iota(jnp.int32, (pad, seq), 0)
            at_lane = lax.broadcasted_iota(jnp.int32, (pad, seq), 1)
            covered = jnp.where((at_row == at_lane) & (row == 1), 1.0, 0.0)
            column = jnp.sum(covered, axis=1, keepdims=True)
            r["mcol"][rows, :] = column
            token = r["token"][...].astype(F32)
            kept = r["pin"][img].astype(F32)
            mixed = jnp.where(column[:seq] > 0.5, token, kept)
            r["x"][image_rows(img, 0, seq), :] = mixed.astype(BF)

        @pl.when(second)
        def _():
            forward_send(img).wait_recv()

        norm_forward(img, r["x"], 0, r["n1"], r["a1"])
        wait_weights(step, range(0, 3))
        for j in range(3):
            projected = dot(r["a1"][rows, :], wg[unit_rows(QKV + j), :], 1, 0)
            if j == 0:
                projected = (projected + r["qv_bias"][0:1, :]) * (1.0 / math.sqrt(width // HEADS))
            if j == 2:
                projected = projected + r["qv_bias"][1:2, :]
            r["qkv"][j, rows, :] = projected.astype(BF)

        def three_pairs(half, carry):
            for pair in range(HEADS // 4):
                attention_forward(img, half * (HEADS // 4) + pair)
            return carry

        lax.fori_loop(0, 2, three_pairs, 0)
        wait_weights(step, range(3, UNITS))
        r["yb"][rows, :] = (
            r["x"][rows, :].astype(F32)
            + dot(r["o"][rows, :], wg[unit_rows(OUT), :], 1, 0)
            + r["out_bias"][...]
        )
        norm_forward(img, r["yb"], 1, r["n2"], r["a2"])
        result = None
        for j in range(4):
            hidden = dot(r["a2"][rows, :], wg[unit_rows(UP + j), :], 1, 0)
            hidden = hidden + r["up_bias"][:, width * j : width * (j + 1)]
            below = 0.5 + 0.5 * lax.erf(hidden * INV_SQRT2)
            slope = below + hidden * (jnp.exp(hidden * hidden * -0.5) * INV_SQRT2PI)
            active = (hidden * below).astype(BF)
            r["act"][j, rows, :] = active
            r["gp"][j, rows, :] = slope.astype(BF)
            term = dot(active, wg[unit_rows(DOWN_W + j), :], 1, 0)
            result = term if result is None else result + term
        r["yb"][rows, :] = r["yb"][rows, :] + result + r["down_bias"][...]

        @pl.when(first)
        def _():
            r["send"][rows, :] = r["yb"][rows, :].astype(BF)
            forward_send(img).start()

        @pl.when(second)
        def _():
            bound_copy(img).start()

    def take_gradient(img):
        @pl.when(first)
        def _():
            backward_send(img).wait_recv()

        @pl.when(second)
        def _():
            tail = image_rows(img, seq // 16 * 16, 16)
            r["dy"][tail, :] = jnp.zeros((16, width), BF)
            r["dy"][image_rows(img, 0, seq), :] = r["pin"][img]

    def norm_backward(img, which, gradient, incoming):
        gain = r["gains"][which : which + 1, :]
        normed = r["n1"] if which == 0 else r["n2"]
        gain_sum = jnp.zeros((8, width), F32)
        shift_sum = jnp.zeros((8, width), F32)
        for b, rows in enumerate(row_blocks(img)):
            here = gradient[16 * b : 16 * (b + 1), :]
            unit = normed[rows, :].astype(F32)
            gain_sum = gain_sum + fold8(here * unit)
            shift_sum = shift_sum + fold8(here)
            scaled = here * gain
            mean = jnp.mean(scaled, axis=1, keepdims=True)
            along = jnp.mean(scaled * unit, axis=1, keepdims=True)
            local = (scaled - mean - unit * along) * r["rstd"][which, rows, :]
            yield b, rows, local + incoming(b, rows)
        r["sm"][which : which + 1, :] += jnp.sum(gain_sum, axis=0, keepdims=True)
        r["sm"][2 + which : 3 + which, :] += jnp.sum(shift_sum, axis=0, keepdims=True)

    def backward_mlp(img):
        rows = image_rows(img)
        incoming = r["dy"][rows, :]
        r["sm"][11:12, :] += jnp.sum(incoming.astype(F32), axis=0, keepdims=True)
        back = None
        for j in range(4):
            change = dot(incoming, wg[unit_rows(DOWN_W + j), :], 1, 1)
            change = change * r["gp"][j, rows, :].astype(F32)
            r["sm"][7 + j : 8 + j, :] += jnp.sum(change, axis=0, keepdims=True)
            narrow = change.astype(BF)
            r["gp"][j, rows, :] = narrow
            term = dot(narrow, wg[unit_rows(UP + j), :], 1, 1)
            back = term if back is None else back + term
        r["tb"][...] = back
        bias_sum = jnp.zeros((8, width), F32)
        for b, block_rows, middle in norm_backward(
            img, 1, r["tb"], lambda b, block_rows: r["dy"][block_rows, :].astype(F32)
        ):
            bias_sum = bias_sum + fold8(middle)
            r["da"][16 * b : 16 * (b + 1), :] = middle
            r["n2"][block_rows, :] = middle.astype(BF)
        r["sm"][6:7, :] += jnp.sum(bias_sum, axis=0, keepdims=True)

    def attention_backward(img, pair):
        rows = image_rows(img)
        lanes = pl.ds(pl.multiple_of(128 * pair, 128), 128)
        queries = halves(r["qkv"][0, rows, lanes])
        keys = r["qkv"][1, rows, lanes]
        values = r["qkv"][2, rows, lanes]
        back = halves(r["do"][:, lanes])
        key_parts = halves(keys)
        d_query = d_key = d_value = None
        for head in range(2):
            prob = r["prob"][img * HEADS + 2 * pair + head]
            wide = prob.astype(F32)
            change = dot(values, back[head], 1, 1)
            carried = jnp.sum(wide * change, axis=0, keepdims=True)
            scores = (wide * (change - carried)).astype(BF)
            terms = (
                dot(scores, key_parts[head], 0, 0),
                dot(scores, queries[head], 1, 0),
                dot(prob, back[head], 1, 0),
            )
            if head == 0:
                d_query, d_key, d_value = terms
            else:
                d_query, d_key, d_value = d_query + terms[0], d_key + terms[1], d_value + terms[2]
        d_query = d_query * (1.0 / math.sqrt(width // HEADS))
        r["sm"][4:5, lanes] += jnp.sum(d_query, axis=0, keepdims=True)
        r["sm"][5:6, lanes] += jnp.sum(d_value, axis=0, keepdims=True)
        r["qkv"][0, rows, lanes] = d_query.astype(BF)
        r["qkv"][1, rows, lanes] = d_key.astype(BF)
        r["qkv"][2, rows, lanes] = d_value.astype(BF)

    def backward_attention(img):
        rows = image_rows(img)
        r["do"][...] = dot(r["n2"][rows, :], wg[unit_rows(OUT), :], 1, 1).astype(BF)

        def three_pairs(half, carry):
            for pair in range(HEADS // 4):
                attention_backward(img, half * (HEADS // 4) + pair)
            return carry

        lax.fori_loop(0, 2, three_pairs, 0)
        back = None
        for j in range(3):
            term = dot(r["qkv"][j, rows, :], wg[unit_rows(QKV + j), :], 1, 1)
            back = term if back is None else back + term
        r["tb"][...] = back
        for b, block_rows, entry in norm_backward(
            img, 0, r["tb"], lambda b, block_rows: r["da"][16 * b : 16 * (b + 1), :]
        ):
            r["da"][16 * b : 16 * (b + 1), :] = entry

        @pl.when(first)
        def _():
            token_sum = jnp.zeros((8, width), F32)
            for b, block_rows in enumerate(row_blocks(img)):
                entry = r["da"][16 * b : 16 * (b + 1), :]
                under = r["mcol"][block_rows, :] > 0.5
                token_sum = token_sum + fold8(jnp.where(under, entry, 0.0))
                r["yb"][block_rows, :] = jnp.where(under, 0.0, entry)
            r["sm"][12:13, :] += jnp.sum(token_sum, axis=0, keepdims=True)
            bound_copy(img).start()

        @pl.when(second)
        def _():
            r["send"][rows, :] = r["da"][...].astype(BF)
            backward_send(img).start()

    if reduce_here:
        mine = [lax.rem(me // bit, 2) for bit in HALVINGS]
        landing = [r["rc"], r["ry"], r["rz"], r["rw"]]
        sends = [r["cs"], r["ys"], r["zs"], r["ws"]]
        arrivals = [r["cr"], r["yr"], r["zr"], r["wr"]]

    def kept_offset(steps):
        offset = 0
        for s in range(steps):
            offset = offset + mine[s] * (width >> (s + 1))
        return offset

    def halving(s, unit):
        size = width >> (s + 1)
        away = kept_offset(s) + (1 - mine[s]) * size
        return pltpu.make_async_remote_copy(
            src_ref=wg.at[unit_rows(unit, away, size), :],
            dst_ref=landing[s].at[pl.ds(pl.multiple_of(unit * size, 16), size), :],
            send_sem=sends[s].at[unit],
            recv_sem=arrivals[s].at[unit],
            device_id=dp_at(HALVINGS[s]),
        )

    def add_arrived(s, unit):
        size = width >> (s + 1)
        halving(s, unit).wait_recv()
        here = kept_offset(s + 1)
        for part in range(size // 48):
            rows = unit_rows(unit, here + 48 * part, 48)
            came = landing[s][pl.ds(pl.multiple_of(unit * size + 48 * part, 16), 48), :]
            both = wg[rows, :].astype(F32) + came.astype(F32)
            if s < 3:
                wg[rows, :] = both.astype(BF)
            else:
                r["grads"][unit] = both * scale
        if s < 3:
            halving(s + 1, unit).start()

    def place(owner):
        where = 0
        for s, bit in enumerate(HALVINGS):
            where = where + lax.rem(owner // bit, 2) * (8 >> s)
        return where

    def weight_gradient(left, right, chunk, first_unit, spread):
        for half in range(2):
            product = dot(left(half), right, 0, 0).astype(BF)
            for b in range(8):
                at = chunk * 16 + 8 * half + b
                if reduce_here:
                    owner, part = at // spread, lax.rem(at, spread)
                    rows = unit_rows(first_unit + part, place(owner) * block, block)
                else:
                    rows = unit_rows(first_unit, at * block, block)
                wg[rows, :] = product[block * b : block * (b + 1), :]

    def half_lanes(half):
        return pl.ds((width // 2) * half, width // 2)

    def down_gradient():
        def one(j, carry):
            weight_gradient(lambda half: r["dy"][:, half_lanes(half)], r["act"][j], 0, j, 1)
            if reduce_here:
                halving(0, j).start()
            return carry

        lax.fori_loop(0, 4, one, 0)

    def start_units(begin, end):
        if reduce_here:
            for unit in range(begin, end):
                halving(0, unit).start()

    def add_units(s, begin, end):
        if reduce_here:

            def one(unit, carry):
                add_arrived(s, unit)
                return carry

            lax.fori_loop(begin, end, one, 0)

    def turn(step, carry):
        img = lax.rem(step, images)
        early = step < images
        back_now = early == second
        down_now = step == jnp.where(first, 2 * images - 1, images)

        @pl.when(early)
        def _():
            forward(step, img)

        @pl.when(back_now)
        def _():
            take_gradient(img)

        @pl.when(down_now)
        def _():
            down_gradient()

        @pl.when(back_now)
        def _():
            backward_mlp(img)

        @pl.when(down_now)
        def _():
            add_units(0, 0, 4)

        @pl.when(back_now)
        def _():
            backward_attention(img)

        return carry

    lax.fori_loop(0, 2 * images, turn, 0)

    def up_one(c, carry):
        weight_gradient(lambda half: r["gp"][c, :, half_lanes(half)], r["a2"][...], c, UP, 4)
        return carry

    lax.fori_loop(0, 4, up_one, 0)
    start_units(UP, OUT)
    weight_gradient(lambda half: r["n2"][:, half_lanes(half)], r["o"][...], 0, OUT, 1)
    start_units(OUT, QKV)
    add_units(0, UP, OUT)

    def qkv_one(c, carry):
        weight_gradient(lambda half: r["qkv"][c, :, half_lanes(half)], r["a1"][...], c, QKV, 3)
        return carry

    lax.fori_loop(0, 3, qkv_one, 0)
    start_units(QKV, UNITS)
    add_units(0, OUT, UNITS)

    if reduce_here:
        hops = [dp_at(bit) for bit in HALVINGS] + [across]

        def small_send(t):
            return pltpu.make_async_remote_copy(
                src_ref=r["sms"].at[t],
                dst_ref=r["smr"].at[t],
                send_sem=r["ss"].at[t],
                recv_sem=r["sr"].at[t],
                device_id=hops[t],
            )

        r["sms"][0] = r["sm"][...]
        small_send(0).start()

        def drain(k, carry):
            @pl.when(k < UNITS)
            def _():
                add_arrived(1, k)

            for t in range(5):

                @pl.when(k == t + 1)
                def _(t=t):
                    small_send(t).wait_recv()
                    if t < 3:
                        r["sms"][t + 1] = r["sms"][t] + r["smr"][t]
                        small_send(t + 1).start()
                    elif t == 3:
                        r["sms"][4] = r["sms"][3] + r["smr"][3]
                        small_send(4).start()
                    else:
                        r["small"][0:12, :] = r["sms"][4, 0:12, :] * scale
                        r["small"][12:SMALL, :] = (
                            r["sms"][4, 12:SMALL, :] + r["smr"][4, 12:SMALL, :]
                        ) * scale

            @pl.when((k >= 1) & (k < UNITS + 1))
            def _():
                add_arrived(2, k - 1)

            @pl.when(k >= 2)
            def _():
                add_arrived(3, k - 2)

            return carry

        lax.fori_loop(0, UNITS + 2, drain, 0)

        def sent(unit, carry):
            for s in range(4):
                halving(s, unit).wait_send()
            return carry

        lax.fori_loop(0, UNITS, sent, 0)
        for t in range(5):
            small_send(t).wait_send()
    else:
        r["small"][...] = r["sm"][...] * scale
        out = pltpu.make_async_copy(wg.at[pl.ds(0, UNITS * width), :], r["grads"], r["pin_sem"])
        out.start()
        out.wait()

    for img in range(images):
        bound_copy(img).wait()

        @pl.when(first)
        def _(img=img):
            forward_send(img).wait_send()

        @pl.when(second)
        def _(img=img):
            backward_send(img).wait_send()


def on_device(n, *args):
    (patches, block_mask, mask_token, norm_gains, norm_shifts, w_qkv, qv_bias, w_out, out_bias) = args[:9]
    w_up, up_bias, w_down, down_bias, cotangent = args[9:]
    images, seq, width = patches.shape
    pad = -(-seq // 16) * 16
    rows = images * pad
    reduce_here = n == 16
    scale = 1.0 / math.sqrt(images * n * seq)
    geo = (n, images, seq, pad, width, scale)
    block = width // 16
    anywhere = pl.BlockSpec(memory_space=pl.ANY)
    vmem = pl.BlockSpec(memory_space=pltpu.VMEM)
    if reduce_here:
        grads_shape = jax.ShapeDtypeStruct((UNITS, block, width), F32)
    else:
        grads_shape = jax.ShapeDtypeStruct((UNITS * width, width), BF)
    narrow = pltpu.VMEM((rows, width), BF)
    dma = pltpu.SemaphoreType.DMA
    scratch = [
        pltpu.VMEM((16 * width, width), BF),
        narrow,
        narrow,
        narrow,
        pltpu.VMEM((3, rows, width), BF),
        narrow,
        narrow,
        narrow,
        pltpu.VMEM((4, rows, width), BF),
        pltpu.VMEM((4, rows, width), BF),
        narrow,
        narrow,
        pltpu.VMEM((images * HEADS, pad, pad), BF),
        pltpu.VMEM((2, rows, 1), F32),
        pltpu.VMEM((rows, 1), F32),
        pltpu.VMEM((rows, width), F32),
        pltpu.VMEM((pad, width), F32),
        pltpu.VMEM((pad, width), F32),
        pltpu.VMEM((pad, width), BF),
        pltpu.VMEM((images, seq, width), BF),
        pltpu.VMEM((SMALL, width), F32),
        pltpu.VMEM((5, SMALL, width), F32),
        pltpu.VMEM((5, SMALL, width), F32),
        dma(()),
        dma((UNITS,)),
        dma((images,)),
        dma((images,)),
        dma((images,)),
        dma((images,)),
        dma((images,)),
    ]
    if reduce_here:
        scratch += [pltpu.VMEM((UNITS * (width >> (s + 1)), width), BF) for s in range(4)]
        scratch += [dma((UNITS,))] * 8 + [dma((5,))] * 2
    weights = 12 * width * width
    bound, grads, small = pl.pallas_call(
        functools.partial(kernel, geo),
        out_shape=(
            jax.ShapeDtypeStruct((images, pad, width), F32),
            grads_shape,
            jax.ShapeDtypeStruct((SMALL, width), F32),
        ),
        in_specs=[anywhere] * 2 + [vmem] * 8 + [anywhere] * 4,
        out_specs=(anywhere, vmem if reduce_here else anywhere, vmem),
        scratch_shapes=scratch,
        compiler_params=pltpu.CompilerParams(
            collective_id=0, has_side_effects=True, vmem_limit_bytes=64 * 1024 * 1024 - 65536
        ),
        cost_estimate=pl.CostEstimate(
            flops=6 * rows * weights, bytes_accessed=4 * weights, transcendentals=rows * width * 8
        ),
        name="relay",
    )(
        patches,
        cotangent,
        block_mask,
        mask_token[None],
        norm_gains[0],
        norm_shifts[0],
        qv_bias[0],
        out_bias,
        up_bias,
        down_bias,
        w_qkv,
        w_out,
        w_up,
        w_down,
    )
    me = lax.axis_index("dp")
    boundary = bound[:, :seq][None]
    share = width // n
    if reduce_here:
        token = small[12]
        vectors = small[:12]
        down = grads[:4].transpose(0, 2, 1).reshape(4 * width, share)
        up = grads[4:8].transpose(2, 0, 1).reshape(width, 4 * share)
        out = grads[8].T
        qkv = grads[9:].transpose(2, 0, 1).reshape(width, 3 * share)
    else:
        token = lax.psum(small[12], ("dp", "section"))
        vectors = lax.psum(small[:12], "dp")
        wide = grads.astype(F32) * scale

        def scattered(first, count):
            part = wide[first * width : (first + count) * width]
            return lax.psum_scatter(part, "dp", scatter_dimension=0, tiled=True).T

        down = lax.psum_scatter(
            wide[: 4 * width].reshape(4, width, width), "dp", scatter_dimension=1, tiled=True
        )
        down = down.transpose(0, 2, 1).reshape(4 * width, share)
        up = scattered(UP, 4)
        out = scattered(OUT, 1)
        qkv = scattered(QKV, 3)

    def cut(first, count):
        return lax.dynamic_slice(vectors, (first, me * share), (count, share))

    up_vector = lax.dynamic_slice(vectors[7:11].reshape(-1), (me * 4 * share,), (4 * share,))
    return (
        boundary,
        token,
        cut(0, 2)[None],
        cut(2, 2)[None],
        qkv[None],
        cut(4, 2)[None],
        out[None],
        cut(6, 1),
        up[None],
        up_vector[None],
        down[None],
        cut(11, 1),
    )


def solution(mesh):
    return jax.shard_map(
        functools.partial(on_device, mesh.shape["dp"]),
        mesh=mesh,
        in_specs=(
            P("dp", None, None),
            P("dp", None),
            P(),
            P("section", None, None),
            P("section", None, None),
            P("section", None, None),
            P("section", None, None),
            P("section", None, None),
            P("section", None),
            P("section", None, None),
            P("section", None),
            P("section", None, None),
            P("section", None),
            P("dp", None, None),
        ),
        out_specs=(
            P("section", "dp", None, None),
            P(),
            P("section", None, "dp"),
            P("section", None, "dp"),
            P("section", None, "dp"),
            P("section", None, "dp"),
            P("section", None, "dp"),
            P("section", "dp"),
            P("section", None, "dp"),
            P("section", "dp"),
            P("section", None, "dp"),
            P("section", "dp"),
        ),
        check_vma=False,
    )
```

time: 1320 us -> 253 us (0.19)
  waiting for transfers between devices: 736 us -> 0 us
  matrix products: 248 us -> 0 us
  Pallas kernels: 0 us -> 234 us
  local copies, waits for them, and re-layouts: 159 us -> 17 us
  other arithmetic: 69.5 us -> 0 us
  blocking collectives: 40 us -> 0 us
  starting transfers between devices: 36.4 us -> 0 us
  between operations: 17.8 us -> 0.67 us
    unnamed x18 -> x0, waiting for transfers between devices: 685 us -> none
    dot_general x65 -> x0, matrix products: 248 us -> none  [the longest x5 41.7 us: mlp_weights(): jnp.einsum('bsf,bsd->fd', active, out_low, preferred_element_type=WIDE)]
    pallas_call x0 -> x1, Pallas kernels: none -> 234 us  [on_device(): pl.pallas_call(functools.partial(kernel, geo), out_shape=(jax.ShapeDtypeS...]
    broadcast_in_dim x6 -> x4, local copies, waits for them, and re-layouts: 62.4 us -> 4.42 us  [the longest x1 1.58 us: on_device(): out[None]]
    ppermute x6 -> x0, waiting for transfers between devices: 51.3 us -> none  [from_behind(): return lax.ppermute(x, axis, pairs)]
    psum x1 -> x0, blocking collectives: 40 us -> none  [on_device(): token_total = lax.psum(token_term, ('dp', 'section'))]
    ppermute x6 -> x0, starting transfers between devices: 35.3 us -> none  [from_behind(): return lax.ppermute(x, axis, pairs)]
    reduce_sum x41 -> x0, other arithmetic: 31.4 us -> none  [the longest x14 11.4 us: normalize(): centered = values - jnp.mean(values, axis=-1, keepdims=True)]
  transfers between devices with their start and end apart: 15 -> 0, of which waited for: 8 -> 0; matrix products, arithmetic and copies ran while one was open for 21% -> 0% of each run, Pallas kernels for 0% -> 0%
where the time goes in v1:
time: 253 us; the launch traced here: 252 us
  Pallas kernels  234 us (92%)
  local copies, waits for them, and re-layouts  17 us (7%)
    pallas_call x1, Pallas kernels, on_device(): pl.pallas_call(functools.partial(kernel, geo), out_shape=(jax.ShapeDtypeS...  234 us

profile of v1, /device:TPU:0, one launch (start us, length us, event | category | flops | bytes accessed | tf_op | source)
XLA Modules:
  0.0 252.1 jit_solution(5512357505876810815)
XLA Ops:
  0.6 1.3 broadcast_in_dim.21.refs_3_
  1.9 234.3 %relay.1 = (f32[3,208,768]{2,1,0:T(8,128)}, f32[12,48,768]{2,1,0:T(8,128)}, f32[16,768]{1,0:T(8,128)}) custom-call(bf16[3,196,768]{2,1,0:T(8,128)(2,1)} %refs_0_.1, bf16[3,196,768]{2,1,0:T(8,128)(2,1)} %refs_1_.1, s32[3,196]{1,0:T(4,128)} %refs_2_.1, bf16[1,768]{1,0:T(2,128)(2,1)} %broadcast_in_dim.21.refs_3_, f32[2,768]{1,0:T(2,128)} %bitcast.34, ...), custom_call_target="tpu_custom_call" | custom-call | flops 26499612672 | bytes 28311552 | tf_op jit(solution)/shard_map/relay/pallas_call | solution.py:618
  236.3 1.5 dynamic-slice_bitcast_fusion
  237.7 1.3 constant_dynamic-slice_fusion
  239.0 0.8 slice.31
  239.8 0.6 dynamic_slice.22
  240.5 2.1 slice_bitcast_fusion.1
  242.6 0.0 copy-start
  242.6 0.4 copy.27
  243.0 1.1 broadcast_in_dim_reshape.11
  244.1 1.8 slice.28
  245.9 1.6 slice_bitcast_fusion.2
  247.5 1.3 slice_reduce_fusion
  248.8 0.0 copy-done
  248.8 0.1 slice_bitcast_fusion
  249.0 3.1 %copy.28 = f32[1,3,196,768]{3,0,2,1:T(1,128)} copy(f32[1,3,196,768]{3,2,1,0:T(8,128)S(1)} %slice_bitcast_fusion) | data formatting | bytes 3612672
  (1 shorter events, 0.0 us)
Async XLA Ops:
  242.6 6.2 %copy-start = (f32[3,208,768]{2,1,0:T(8,128)S(1)}, f32[3,208,768]{2,1,0:T(8,128)}, u32[]{:S(2)}) copy-start(f32[3,208,768]{2,1,0:T(8,128)} %get-tuple-element.15) | copy-start | bytes 5750788

commit v2 on v1

--- a/solution.py
+++ b/solution.py
@@ -12,7 +12,8 @@
 EPS = 1e-06
 BF = jnp.bfloat16
 F32 = jnp.float32
-HALVINGS = (1, 2, 8, 4)
+Z_FIRST = (2, 4)
+WINDOW = 2
 UNITS = 12
 UP, OUT, QKV, DOWN_W = 4, 8, 9, 12
 SMALL = 16
@@ -37,11 +38,17 @@
     total_rows = images * pad
     block = width // 16
     names = ["patches", "cotangent", "mask", "token", "gains", "shifts", "qv_bias", "out_bias", "up_bias"]
-    names += ["down_bias", "w_qkv", "w_out", "w_up", "w_down", "bound", "grads", "small", "wg", "x", "n1"]
-    names += ["a1", "qkv", "o", "n2", "a2", "act", "gp", "dy", "send", "prob", "rstd", "mcol", "yb", "da"]
-    names += ["tb", "do", "pin", "sm", "sms", "smr", "pin_sem", "w_sem", "out_sem", "fs", "fr", "bs", "br"]
+    names += ["down_bias", "w_qkv", "w_out", "w_up", "w_down", "bound"]
     if reduce_here:
-        names += ["rc", "ry", "rz", "rw", "cs", "cr", "ys", "yr", "zs", "zr", "ws", "wr", "ss", "sr"]
+        names += ["down", "up", "out", "three", "g_gains", "g_shifts", "g_qv", "g_out", "g_up", "g_down"]
+        names += ["g_token"]
+    else:
+        names += ["grads", "small"]
+    names += ["wg", "x", "n1", "a1", "qkv", "o", "n2", "a2", "act", "gp", "dy", "send", "prob", "cols"]
+    names += ["yb", "da", "tb", "do", "pin", "plain", "sm", "sms", "smr"]
+    names += ["pin_sem", "w_sem", "out_sem", "fs", "fr", "bs", "br"]
+    if reduce_here:
+        names += ["rc", "ry", "zb", "zf", "cs", "cr", "ys", "yr", "rs", "rr", "ls", "lr", "ss", "sr"]
     r = dict(zip(names, refs, strict=True))
     wg = r["wg"]
     me = lax.axis_index("dp")
@@ -53,7 +60,11 @@
         return {"dp": me + bit - 2 * bit * mine, "section": sec}
 
     across = {"dp": me, "section": 1 - sec}
-    partners = [across] + ([dp_at(bit) for bit in HALVINGS] if reduce_here else [])
+    core, y_at, z_at = lax.rem(me, 2), lax.rem(me // 2, 2), me // 4
+    partners = [across]
+    if reduce_here:
+        partners += [dp_at(1), dp_at(2)]
+        partners += [{"dp": lax.rem(me + 4 * turn, n), "section": sec} for turn in (1, 2, 3)]
 
     def unit_rows(unit, offset=0, size=width):
         return pl.ds(pl.multiple_of(unit * width + offset, 16), size)
@@ -114,24 +125,25 @@
         )
 
     def bound_copy(img):
-        rows = image_rows(img)
-        return pltpu.make_async_copy(
-            r["yb"].at[rows, :], r["bound"].at[img], r["out_sem"].at[img]
-        )
+        return pltpu.make_async_copy(r["plain"].at[img], r["bound"].at[img], r["out_sem"].at[img])
+
+    def write_bound(img, at, values):
+        size = min(16, seq - at)
+        r["plain"][img, at : at + size, 0, :] = values[:size]
 
     def row_blocks(img):
         return [image_rows(img, 16 * b, 16) for b in range(pad // 16)]
 
-    def norm_forward(img, source, which, normed, scaled):
+    def norm_forward(img, read, which, normed, scaled):
         gain = r["gains"][which : which + 1, :]
         shift = r["shifts"][which : which + 1, :]
-        for rows in row_blocks(img):
-            values = source[rows, :].astype(F32)
+        for b, rows in enumerate(row_blocks(img)):
+            values = read(b, rows)
             centered = values - jnp.mean(values, axis=1, keepdims=True)
             variance = jnp.mean(centered * centered, axis=1, keepdims=True)
             inverse = lax.rsqrt(variance + EPS)
             unit = centered * inverse
-            r["rstd"][which, rows, :] = inverse
+            r["cols"][rows, which : which + 1] = inverse
             normed[rows, :] = unit.astype(BF)
             scaled[rows, :] = (unit * gain + shift).astype(BF)
 
@@ -178,8 +190,8 @@
             at_lane = lax.broadcasted_iota(jnp.int32, (pad, seq), 1)
             covered = jnp.where((at_row == at_lane) & (row == 1), 1.0, 0.0)
             column = jnp.sum(covered, axis=1, keepdims=True)
-            r["mcol"][rows, :] = column
-            token = r["token"][...].astype(F32)
+            r["cols"][rows, 2:3] = column
+            token = r["token"][...][None, :].astype(F32)
             kept = r["pin"][img].astype(F32)
             mixed = jnp.where(column[:seq] > 0.5, token, kept)
             r["x"][image_rows(img, 0, seq), :] = mixed.astype(BF)
@@ -188,7 +200,7 @@
         def _():
             forward_send(img).wait_recv()
 
-        norm_forward(img, r["x"], 0, r["n1"], r["a1"])
+        norm_forward(img, lambda b, at: r["x"][at, :].astype(F32), 0, r["n1"], r["a1"])
         wait_weights(step, range(0, 3))
         for j in range(3):
             projected = dot(r["a1"][rows, :], wg[unit_rows(QKV + j), :], 1, 0)
@@ -205,12 +217,12 @@
 
         lax.fori_loop(0, 2, three_pairs, 0)
         wait_weights(step, range(3, UNITS))
-        r["yb"][rows, :] = (
+        r["yb"][...] = (
             r["x"][rows, :].astype(F32)
             + dot(r["o"][rows, :], wg[unit_rows(OUT), :], 1, 0)
             + r["out_bias"][...]
         )
-        norm_forward(img, r["yb"], 1, r["n2"], r["a2"])
+        norm_forward(img, lambda b, at: r["yb"][16 * b : 16 * (b + 1), :], 1, r["n2"], r["a2"])
         result = None
         for j in range(4):
             hidden = dot(r["a2"][rows, :], wg[unit_rows(UP + j), :], 1, 0)
@@ -222,16 +234,17 @@
             r["gp"][j, rows, :] = slope.astype(BF)
             term = dot(active, wg[unit_rows(DOWN_W + j), :], 1, 0)
             result = term if result is None else result + term
-        r["yb"][rows, :] = r["yb"][rows, :] + result + r["down_bias"][...]
+        result = r["yb"][...] + result + r["down_bias"][...]
 
         @pl.when(first)
         def _():
-            r["send"][rows, :] = r["yb"][rows, :].astype(BF)
+            r["send"][rows, :] = result.astype(BF)
             forward_send(img).start()
 
         @pl.when(second)
         def _():
-            bound_copy(img).start()
+            for at in range(0, seq, 16):
+                write_bound(img, at, result[at : at + 16])
 
     def take_gradient(img):
         @pl.when(first)
@@ -257,7 +270,7 @@
             scaled = here * gain
             mean = jnp.mean(scaled, axis=1, keepdims=True)
             along = jnp.mean(scaled * unit, axis=1, keepdims=True)
-            local = (scaled - mean - unit * along) * r["rstd"][which, rows, :]
+            local = (scaled - mean - unit * along) * r["cols"][rows, which : which + 1]
             yield b, rows, local + incoming(b, rows)
         r["sm"][which : which + 1, :] += jnp.sum(gain_sum, axis=0, keepdims=True)
         r["sm"][2 + which : 3 + which, :] += jnp.sum(shift_sum, axis=0, keepdims=True)
@@ -285,44 +298,43 @@
             r["n2"][block_rows, :] = middle.astype(BF)
         r["sm"][6:7, :] += jnp.sum(bias_sum, axis=0, keepdims=True)
 
-    def attention_backward(img, pair):
+    def attention_backward(img, pairs):
         rows = image_rows(img)
-        lanes = pl.ds(pl.multiple_of(128 * pair, 128), 128)
-        queries = halves(r["qkv"][0, rows, lanes])
-        keys = r["qkv"][1, rows, lanes]
-        values = r["qkv"][2, rows, lanes]
-        back = halves(r["do"][:, lanes])
-        key_parts = halves(keys)
-        d_query = d_key = d_value = None
-        for head in range(2):
-            prob = r["prob"][img * HEADS + 2 * pair + head]
-            wide = prob.astype(F32)
-            change = dot(values, back[head], 1, 1)
-            carried = jnp.sum(wide * change, axis=0, keepdims=True)
-            scores = (wide * (change - carried)).astype(BF)
-            terms = (
-                dot(scores, key_parts[head], 0, 0),
-                dot(scores, queries[head], 1, 0),
-                dot(prob, back[head], 1, 0),
-            )
-            if head == 0:
-                d_query, d_key, d_value = terms
-            else:
-                d_query, d_key, d_value = d_query + terms[0], d_key + terms[1], d_value + terms[2]
-        d_query = d_query * (1.0 / math.sqrt(width // HEADS))
-        r["sm"][4:5, lanes] += jnp.sum(d_query, axis=0, keepdims=True)
-        r["sm"][5:6, lanes] += jnp.sum(d_value, axis=0, keepdims=True)
-        r["qkv"][0, rows, lanes] = d_query.astype(BF)
-        r["qkv"][1, rows, lanes] = d_key.astype(BF)
-        r["qkv"][2, rows, lanes] = d_value.astype(BF)
+        places = [pl.ds(pl.multiple_of(128 * pair, 128), 128) for pair in pairs]
+        loaded = []
+        for pair, lanes in zip(pairs, places):
+            probs = [r["prob"][img * HEADS + 2 * pair + head] for head in range(2)]
+            loaded.append((*[r["qkv"][i, rows, lanes] for i in range(3)], r["do"][:, lanes], probs))
+        results = []
+        for queries, keys, values, back, probs in loaded:
+            query_parts, key_parts, back_parts = halves(queries), halves(keys), halves(back)
+            total = None
+            for head in range(2):
+                wide = probs[head].astype(F32)
+                change = dot(values, back_parts[head], 1, 1)
+                carried = jnp.sum(wide * change, axis=0, keepdims=True)
+                scores = (wide * (change - carried)).astype(BF)
+                terms = (
+                    dot(scores, key_parts[head], 0, 0),
+                    dot(scores, query_parts[head], 1, 0),
+                    dot(probs[head], back_parts[head], 1, 0),
+                )
+                total = terms if total is None else [a + b for a, b in zip(total, terms)]
+            d_query, d_key, d_value = total
+            results.append((d_query * (1.0 / math.sqrt(width // HEADS)), d_key, d_value))
+        for (d_query, d_key, d_value), lanes in zip(results, places):
+            r["sm"][4:5, lanes] += jnp.sum(d_query, axis=0, keepdims=True)
+            r["sm"][5:6, lanes] += jnp.sum(d_value, axis=0, keepdims=True)
+            r["qkv"][0, rows, lanes] = d_query.astype(BF)
+            r["qkv"][1, rows, lanes] = d_key.astype(BF)
+            r["qkv"][2, rows, lanes] = d_value.astype(BF)
 
     def backward_attention(img):
         rows = image_rows(img)
         r["do"][...] = dot(r["n2"][rows, :], wg[unit_rows(OUT), :], 1, 1).astype(BF)
 
         def three_pairs(half, carry):
-            for pair in range(HEADS // 4):
-                attention_backward(img, half * (HEADS // 4) + pair)
+            attention_backward(img, [half * (HEADS // 4) + pair for pair in range(HEADS // 4)])
             return carry
 
         lax.fori_loop(0, 2, three_pairs, 0)
@@ -341,69 +353,184 @@
             token_sum = jnp.zeros((8, width), F32)
             for b, block_rows in enumerate(row_blocks(img)):
                 entry = r["da"][16 * b : 16 * (b + 1), :]
-                under = r["mcol"][block_rows, :] > 0.5
+                under = r["cols"][block_rows, 2:3] > 0.5
                 token_sum = token_sum + fold8(jnp.where(under, entry, 0.0))
-                r["yb"][block_rows, :] = jnp.where(under, 0.0, entry)
+                if 16 * b < seq:
+                    write_bound(img, 16 * b, jnp.where(under, 0.0, entry))
             r["sm"][12:13, :] += jnp.sum(token_sum, axis=0, keepdims=True)
-            bound_copy(img).start()
 
         @pl.when(second)
         def _():
             r["send"][rows, :] = r["da"][...].astype(BF)
             backward_send(img).start()
 
-    if reduce_here:
-        mine = [lax.rem(me // bit, 2) for bit in HALVINGS]
-        landing = [r["rc"], r["ry"], r["rz"], r["rw"]]
-        sends = [r["cs"], r["ys"], r["zs"], r["ws"]]
-        arrivals = [r["cr"], r["yr"], r["zr"], r["wr"]]
-
-    def kept_offset(steps):
-        offset = 0
-        for s in range(steps):
-            offset = offset + mine[s] * (width >> (s + 1))
-        return offset
-
-    def halving(s, unit):
-        size = width >> (s + 1)
-        away = kept_offset(s) + (1 - mine[s]) * size
+    half_rows, quarter = width // 2, width // 4
+    across_core, across_y = dp_at(1), dp_at(2)
+
+    def core_copy(unit):
+        return pltpu.make_async_remote_copy(
+            src_ref=wg.at[unit_rows(unit, half_rows * (1 - core), half_rows), :],
+            dst_ref=r["rc"].at[pl.ds(pl.multiple_of(unit * half_rows, 16), half_rows), :],
+            send_sem=r["cs"].at[unit],
+            recv_sem=r["cr"].at[unit],
+            device_id=across_core,
+        )
+
+    def y_slot(unit, z_first):
+        if z_first:
+            at = (UNITS - Z_FIRST[1] + Z_FIRST[0]) * quarter + (unit - Z_FIRST[0]) * block
+            return r["ry"].at[pl.ds(pl.multiple_of(at, 16), block), :]
+        return r["ry"].at[pl.ds(pl.multiple_of(index_of(unit) * quarter, 16), quarter), :]
+
+    def index_of(unit):
+        return jnp.where(unit < Z_FIRST[0], unit, unit - (Z_FIRST[1] - Z_FIRST[0]))
+
+    def y_copy(unit, z_first):
+        if z_first:
+            size, away = block, half_rows * core + 2 * block * z_at + block * (1 - y_at)
+        else:
+            size, away = quarter, half_rows * core + quarter * (1 - y_at)
         return pltpu.make_async_remote_copy(
             src_ref=wg.at[unit_rows(unit, away, size), :],
-            dst_ref=landing[s].at[pl.ds(pl.multiple_of(unit * size, 16), size), :],
-            send_sem=sends[s].at[unit],
-            recv_sem=arrivals[s].at[unit],
-            device_id=dp_at(HALVINGS[s]),
+            dst_ref=y_slot(unit, z_first),
+            send_sem=r["ys"].at[unit],
+            recv_sem=r["yr"].at[unit],
+            device_id=across_y,
         )
 
-    def add_arrived(s, unit):
-        size = width >> (s + 1)
-        halving(s, unit).wait_recv()
-        here = kept_offset(s + 1)
-        for part in range(size // 48):
-            rows = unit_rows(unit, here + 48 * part, 48)
-            came = landing[s][pl.ds(pl.multiple_of(unit * size + 48 * part, 16), 48), :]
-            both = wg[rows, :].astype(F32) + came.astype(F32)
-            if s < 3:
-                wg[rows, :] = both.astype(BF)
+    def z_rows(unit, owner, z_first):
+        if z_first:
+            return unit_rows(unit, half_rows * core + 2 * block * owner, 2 * block)
+        return unit_rows(unit, half_rows * core + quarter * y_at + block * owner, block)
+
+    def z_slot(unit, slot, z_first):
+        if z_first:
+            at = (unit - Z_FIRST[0]) * 10 * block + slot * 2 * block
+            return r["zf"].at[pl.ds(pl.multiple_of(at, 16), 2 * block), :]
+        at = index_of(unit) * 5 * block + slot * block
+        return r["zb"].at[pl.ds(pl.multiple_of(at, 16), block), :]
+
+    def z_copy(unit, owner, toward, z_first, goes_to):
+        up = toward > 0
+        slot = owner if up or owner != goes_to else 4
+        return pltpu.make_async_remote_copy(
+            src_ref=wg.at[z_rows(unit, owner, z_first), :],
+            dst_ref=z_slot(unit, slot, z_first),
+            send_sem=r["rs" if up else "ls"].at[unit * 4 + owner],
+            recv_sem=r["rr" if up else "lr"].at[unit * 4 + owner],
+            device_id={"dp": lax.rem(me + n + 4 * toward, n), "section": sec},
+        )
+
+    def add_rows(unit, offset, source, size):
+        for part in range(size // block):
+            rows = unit_rows(unit, offset + block * part, block)
+            came = source[block * part : block * (part + 1), :]
+            wg[rows, :] = (wg[rows, :].astype(F32) + came.astype(F32)).astype(BF)
+
+    def add_core(unit, z_first):
+        core_copy(unit).wait_recv()
+        came = r["rc"].at[pl.ds(pl.multiple_of(unit * half_rows, 16), half_rows), :]
+        add_rows(unit, half_rows * core, came, half_rows)
+        if z_first:
+            z_start(unit, True)
+        else:
+            y_copy(unit, False).start()
+
+    def z_start(unit, z_first):
+        @pl.when(z_at == 0)
+        def _():
+            for owner in (3, 2, 1):
+                z_copy(unit, owner, 1, z_first, 1).start()
+
+        @pl.when(z_at == 3)
+        def _():
+            for owner in (0, 1, 2):
+                z_copy(unit, owner, -1, z_first, 2).start()
+
+    def z_hop(hop, unit, z_first):
+        size = 2 * block if z_first else block
+
+        def pass_on(here, owner, toward):
+            z_copy(unit, owner, toward, z_first, here).wait_recv()
+            rows = z_rows(unit, owner, z_first)
+            came = z_slot(unit, owner, z_first)
+            wg[rows, :] = (wg[rows, :].astype(F32) + came[...].astype(F32)).astype(BF)
+            z_copy(unit, owner, toward, z_first, here + toward).start()
+
+        def finish(here):
+            total = wg[z_rows(unit, here, z_first), :].astype(F32)
+            if here > 0:
+                z_copy(unit, here, 1, z_first, here).wait_recv()
+                total = total + z_slot(unit, here, z_first)[...].astype(F32)
+            if here < 3:
+                z_copy(unit, here, -1, z_first, here).wait_recv()
+                total = total + z_slot(unit, 4, z_first)[...].astype(F32)
+            if z_first:
+                wg[z_rows(unit, here, True), :] = total.astype(BF)
+                y_copy(unit, True).start()
             else:
-                r["grads"][unit] = both * scale
-        if s < 3:
-            halving(s + 1, unit).start()
-
-    def place(owner):
-        where = 0
-        for s, bit in enumerate(HALVINGS):
-            where = where + lax.rem(owner // bit, 2) * (8 >> s)
-        return where
-
-    def weight_gradient(left, right, chunk, first_unit, spread):
+                put(unit, total)
+
+        @pl.when(z_at == hop)
+        def _():
+            for owner in range(3, hop, -1):
+                pass_on(hop, owner, 1)
+            if hop >= 2:
+                finish(hop)
+
+        @pl.when(z_at == 3 - hop)
+        def _():
+            for owner in range(3 - hop):
+                pass_on(3 - hop, owner, -1)
+            if hop >= 2:
+                finish(3 - hop)
+
+    def put(unit, total):
+        total = total * scale
+
+        @pl.when(unit < UP)
+        def _():
+            r["down"][:, pl.ds(pl.multiple_of(jnp.minimum(unit, 3) * width, 128), width)] = total
+
+        @pl.when((unit >= UP) & (unit < OUT))
+        def _():
+            r["up"][pl.ds(pl.multiple_of(jnp.clip(unit - UP, 0, 3) * block, 16), block), :] = total
+
+        @pl.when(unit == OUT)
+        def _():
+            r["out"][...] = total
+
+        @pl.when(unit >= QKV)
+        def _():
+            r["three"][pl.ds(pl.multiple_of(jnp.clip(unit - QKV, 0, 2) * block, 16), block), :] = total
+
+    def finish_z_first(unit):
+        y_copy(unit, True).wait_recv()
+        mine = unit_rows(unit, half_rows * core + 2 * block * z_at + block * y_at, block)
+        came = y_slot(unit, True)[...]
+        put(unit, wg[mine, :].astype(F32) + came.astype(F32))
+
+    def add_y(unit):
+        y_copy(unit, False).wait_recv()
+        add_rows(unit, half_rows * core + quarter * y_at, y_slot(unit, False), quarter)
+        z_start(unit, False)
+
+    def place(owner, z_first):
+        core_of, y_of, z_of = lax.rem(owner, 2), lax.rem(owner // 2, 2), owner // 4
+        if z_first:
+            return core_of * 8 + z_of * 2 + y_of
+        return core_of * 8 + y_of * 4 + z_of
+
+    def weight_gradient(left, right, chunk, first_unit, spread, z_first=False):
         for half in range(2):
             product = dot(left(half), right, 0, 0).astype(BF)
             for b in range(8):
                 at = chunk * 16 + 8 * half + b
+                if spread == 1:
+                    at = 8 * half + b
                 if reduce_here:
                     owner, part = at // spread, lax.rem(at, spread)
-                    rows = unit_rows(first_unit + part, place(owner) * block, block)
+                    rows = unit_rows(first_unit + part, place(owner, z_first) * block, block)
                 else:
                     rows = unit_rows(first_unit, at * block, block)
                 wg[rows, :] = product[block * b : block * (b + 1), :]
@@ -412,27 +539,44 @@
         return pl.ds((width // 2) * half, width // 2)
 
     def down_gradient():
-        def one(j, carry):
-            weight_gradient(lambda half: r["dy"][:, half_lanes(half)], r["act"][j], 0, j, 1)
-            if reduce_here:
-                halving(0, j).start()
-            return carry
-
-        lax.fori_loop(0, 4, one, 0)
+        def one(z_first):
+            def body(j, carry):
+                weight_gradient(
+                    lambda half: r["dy"][:, half_lanes(half)], r["act"][j], j, j, 1, z_first
+                )
+                if reduce_here:
+                    core_copy(j).start()
+
+                    @pl.when(j > 0)
+                    def _():
+                        if z_first:
+                            pl.when(j == Z_FIRST[0])(lambda: add_core(j - 1, False))
+                            pl.when(j > Z_FIRST[0])(lambda: add_core(j - 1, True))
+                        else:
+                            add_core(j - 1, False)
+
+                return carry
+
+            return body
+
+        lax.fori_loop(0, Z_FIRST[0], one(False), 0)
+        lax.fori_loop(*Z_FIRST, one(True), 0)
+        if reduce_here:
+            add_core(Z_FIRST[1] - 1, True)
 
     def start_units(begin, end):
         if reduce_here:
             for unit in range(begin, end):
-                halving(0, unit).start()
-
-    def add_units(s, begin, end):
+                core_copy(unit).start()
+
+    def z_first_hops(hop):
         if reduce_here:
 
             def one(unit, carry):
-                add_arrived(s, unit)
+                z_hop(hop, unit, True)
                 return carry
 
-            lax.fori_loop(begin, end, one, 0)
+            lax.fori_loop(*Z_FIRST, one, 0)
 
     def turn(step, carry):
         img = lax.rem(step, images)
@@ -456,9 +600,9 @@
         def _():
             backward_mlp(img)
 
-        @pl.when(down_now)
-        def _():
-            add_units(0, 0, 4)
+        @pl.when(down_now & first)
+        def _():
+            z_first_hops(1)
 
         @pl.when(back_now)
         def _():
@@ -474,9 +618,17 @@
 
     lax.fori_loop(0, 4, up_one, 0)
     start_units(UP, OUT)
+    if reduce_here:
+        for unit in range(UP, UP + WINDOW):
+            add_core(unit, False)
+
+    @pl.when(second)
+    def _():
+        z_first_hops(1)
+
+    z_first_hops(2)
     weight_gradient(lambda half: r["n2"][:, half_lanes(half)], r["o"][...], 0, OUT, 1)
     start_units(OUT, QKV)
-    add_units(0, UP, OUT)
 
     def qkv_one(c, carry):
         weight_gradient(lambda half: r["qkv"][c, :, half_lanes(half)], r["a1"][...], c, QKV, 3)
@@ -484,10 +636,13 @@
 
     lax.fori_loop(0, 3, qkv_one, 0)
     start_units(QKV, UNITS)
-    add_units(0, OUT, UNITS)
+    z_first_hops(3)
+
+    for img in range(images):
+        bound_copy(img).start()
 
     if reduce_here:
-        hops = [dp_at(bit) for bit in HALVINGS] + [across]
+        hops = [dp_at(1), dp_at(2), dp_at(8), dp_at(4), across]
 
         def small_send(t):
             return pltpu.make_async_remote_copy(
@@ -500,47 +655,83 @@
 
         r["sms"][0] = r["sm"][...]
         small_send(0).start()
+        in_order = UNITS - (Z_FIRST[1] - Z_FIRST[0])
+
+        def unit_at(index):
+            return jnp.where(index < Z_FIRST[0], index, index + Z_FIRST[1] - Z_FIRST[0])
+
+        def small_step(t):
+            small_send(t).wait_recv()
+            if t < 4:
+                r["sms"][t + 1] = r["sms"][t] + r["smr"][t]
+                small_send(t + 1).start()
+                return
+            total = r["sms"][4] * scale
+            shift = lax.rem(width - block * me, width)
+            turned = pltpu.roll(total, shift, 1)[:, :block]
+            r["g_gains"][0] = turned[0:2]
+            r["g_shifts"][0] = turned[2:4]
+            r["g_qv"][0] = turned[4:6]
+            r["g_out"][...] = turned[6:7]
+            r["g_down"][...] = turned[11:12]
+            up_row = r["sms"][4, pl.ds(7 + me // 4, 1), :] * scale
+            up_shift = lax.rem(width - 4 * block * lax.rem(me, 4), width)
+            spread_row = jnp.broadcast_to(up_row, (8, width))
+            r["g_up"][...] = pltpu.roll(spread_row, up_shift, 1)[0:1, : 4 * block]
+            token = (r["sms"][4, 12:13, :] + r["smr"][4, 12:13, :]) * scale
+            r["g_token"][...] = token.reshape(width)
 
         def drain(k, carry):
-            @pl.when(k < UNITS)
+            @pl.when(k < in_order)
             def _():
-                add_arrived(1, k)
+                add_y(unit_at(k))
+
+            @pl.when((k >= Z_FIRST[0]) & (k + WINDOW < in_order))
+            def _():
+                add_core(unit_at(k + WINDOW), False)
+
+            for hop in (1, 2, 3):
+
+                @pl.when((k >= hop) & (k < in_order + hop))
+                def _(hop=hop):
+                    z_hop(hop, unit_at(k - hop), False)
 
             for t in range(5):
 
                 @pl.when(k == t + 1)
                 def _(t=t):
-                    small_send(t).wait_recv()
-                    if t < 3:
-                        r["sms"][t + 1] = r["sms"][t] + r["smr"][t]
-                        small_send(t + 1).start()
-                    elif t == 3:
-                        r["sms"][4] = r["sms"][3] + r["smr"][3]
-                        small_send(4).start()
-                    else:
-                        r["small"][0:12, :] = r["sms"][4, 0:12, :] * scale
-                        r["small"][12:SMALL, :] = (
-                            r["sms"][4, 12:SMALL, :] + r["smr"][4, 12:SMALL, :]
-                        ) * scale
-
-            @pl.when((k >= 1) & (k < UNITS + 1))
+                    small_step(t)
+
+            @pl.when(k == 2)
             def _():
-                add_arrived(2, k - 1)
-
-            @pl.when(k >= 2)
-            def _():
-                add_arrived(3, k - 2)
+                for unit in range(*Z_FIRST):
+                    finish_z_first(unit)
 
             return carry
 
-        lax.fori_loop(0, UNITS + 2, drain, 0)
-
-        def sent(unit, carry):
-            for s in range(4):
-                halving(s, unit).wait_send()
-            return carry
-
-        lax.fori_loop(0, UNITS, sent, 0)
+        lax.fori_loop(0, in_order + 3, drain, 0)
+
+        def sent(z_first):
+            def body(unit, carry):
+                core_copy(unit).wait_send()
+                y_copy(unit, z_first).wait_send()
+                for here in range(4):
+
+                    @pl.when(z_at == here)
+                    def _(here=here):
+                        for owner in range(4):
+                            if owner > here:
+                                z_copy(unit, owner, 1, z_first, here + 1).wait_send()
+                            if owner < here:
+                                z_copy(unit, owner, -1, z_first, here - 1).wait_send()
+
+                return carry
+
+            return body
+
+        lax.fori_loop(0, Z_FIRST[0], sent(False), 0)
+        lax.fori_loop(*Z_FIRST, sent(True), 0)
+        lax.fori_loop(Z_FIRST[1], UNITS, sent(False), 0)
         for t in range(5):
             small_send(t).wait_send()
     else:
@@ -559,6 +750,20 @@
         @pl.when(second)
         def _(img=img):
             backward_send(img).wait_send()
+
+
+def hand_on(count, *refs):
+    given, results, held = refs[:count], refs[count : 2 * count], refs[2 * count : 3 * count]
+    sems = refs[-1]
+    loads = [pltpu.make_async_copy(given[i], held[i], sems.at[0, i]) for i in range(count)]
+    stores = [pltpu.make_async_copy(held[i], results[i], sems.at[1, i]) for i in range(count)]
+    for load in loads:
+        load.start()
+    for load, store in zip(loads, stores):
+        load.wait()
+        store.start()
+    for store in stores:
+        store.wait()
 
 
 def on_device(n, *args):
@@ -573,10 +778,17 @@
     block = width // 16
     anywhere = pl.BlockSpec(memory_space=pl.ANY)
     vmem = pl.BlockSpec(memory_space=pltpu.VMEM)
+    shapes = [(images, seq, 1, width)]
     if reduce_here:
-        grads_shape = jax.ShapeDtypeStruct((UNITS, block, width), F32)
+        shapes += [(block, 4 * width), (4 * block, width), (block, width), (3 * block, width)]
+        shapes += [(1, 2, block)] * 3 + [(1, block), (1, 4 * block), (1, block), (width,)]
+        out_shape = [jax.ShapeDtypeStruct(shape, F32) for shape in shapes]
     else:
-        grads_shape = jax.ShapeDtypeStruct((UNITS * width, width), BF)
+        out_shape = [
+            jax.ShapeDtypeStruct(shapes[0], F32),
+            jax.ShapeDtypeStruct((UNITS * width, width), BF),
+            jax.ShapeDtypeStruct((SMALL, width), F32),
+        ]
     narrow = pltpu.VMEM((rows, width), BF)
     dma = pltpu.SemaphoreType.DMA
     scratch = [
@@ -593,13 +805,13 @@
         narrow,
         narrow,
         pltpu.VMEM((images * HEADS, pad, pad), BF),
-        pltpu.VMEM((2, rows, 1), F32),
-        pltpu.VMEM((rows, 1), F32),
-        pltpu.VMEM((rows, width), F32),
+        pltpu.VMEM((rows, 3), F32),
+        pltpu.VMEM((pad, width), F32),
         pltpu.VMEM((pad, width), F32),
         pltpu.VMEM((pad, width), F32),
         pltpu.VMEM((pad, width), BF),
         pltpu.VMEM((images, seq, width), BF),
+        pltpu.VMEM((images, seq, 1, width), F32),
         pltpu.VMEM((SMALL, width), F32),
         pltpu.VMEM((5, SMALL, width), F32),
         pltpu.VMEM((5, SMALL, width), F32),
@@ -612,18 +824,20 @@
         dma((images,)),
     ]
     if reduce_here:
-        scratch += [pltpu.VMEM((UNITS * (width >> (s + 1)), width), BF) for s in range(4)]
-        scratch += [dma((UNITS,))] * 8 + [dma((5,))] * 2
+        z_first = Z_FIRST[1] - Z_FIRST[0]
+        scratch += [
+            pltpu.VMEM((UNITS * width // 2, width), BF),
+            pltpu.VMEM((((UNITS - z_first) * 4 + z_first) * block, width), BF),
+            pltpu.VMEM(((UNITS - z_first) * 5 * block, width), BF),
+            pltpu.VMEM((z_first * 10 * block, width), BF),
+        ]
+        scratch += [dma((UNITS,))] * 4 + [dma((UNITS * 4,))] * 4 + [dma((5,))] * 2
     weights = 12 * width * width
-    bound, grads, small = pl.pallas_call(
+    results = pl.pallas_call(
         functools.partial(kernel, geo),
-        out_shape=(
-            jax.ShapeDtypeStruct((images, pad, width), F32),
-            grads_shape,
-            jax.ShapeDtypeStruct((SMALL, width), F32),
-        ),
+        out_shape=out_shape,
         in_specs=[anywhere] * 2 + [vmem] * 8 + [anywhere] * 4,
-        out_specs=(anywhere, vmem if reduce_here else anywhere, vmem),
+        out_specs=[anywhere] + ([vmem] * 11 if reduce_here else [anywhere, vmem]),
         scratch_shapes=scratch,
         compiler_params=pltpu.CompilerParams(
             collective_id=0, has_side_effects=True, vmem_limit_bytes=64 * 1024 * 1024 - 65536
@@ -636,7 +850,7 @@
         patches,
         cotangent,
         block_mask,
-        mask_token[None],
+        mask_token,
         norm_gains[0],
         norm_shifts[0],
         qv_bias[0],
@@ -648,51 +862,46 @@
         w_up,
         w_down,
     )
+    if reduce_here:
+        count = len(out_shape)
+        results = pl.pallas_call(
+            functools.partial(hand_on, count),
+            out_shape=out_shape,
+            in_specs=[anywhere] * count,
+            out_specs=[anywhere] * count,
+            scratch_shapes=[pltpu.VMEM(a.shape, a.dtype) for a in out_shape] + [dma((2, count))],
+            name="hand_on",
+        )(*results)
+        bound, down, up, out, qkv, gains, shifts, qv, out_vector, up_vector, down_vector, token = results
+        boundary = bound.transpose(2, 0, 1, 3)
+        parts = (boundary, token, gains, shifts, qkv.T[None], qv, out.T[None], out_vector, up.T[None])
+        return (*parts, up_vector, down.reshape(block, 4 * width).T[None], down_vector)
+    bound, grads, small = results
     me = lax.axis_index("dp")
-    boundary = bound[:, :seq][None]
     share = width // n
-    if reduce_here:
-        token = small[12]
-        vectors = small[:12]
-        down = grads[:4].transpose(0, 2, 1).reshape(4 * width, share)
-        up = grads[4:8].transpose(2, 0, 1).reshape(width, 4 * share)
-        out = grads[8].T
-        qkv = grads[9:].transpose(2, 0, 1).reshape(width, 3 * share)
-    else:
-        token = lax.psum(small[12], ("dp", "section"))
-        vectors = lax.psum(small[:12], "dp")
-        wide = grads.astype(F32) * scale
-
-        def scattered(first, count):
-            part = wide[first * width : (first + count) * width]
-            return lax.psum_scatter(part, "dp", scatter_dimension=0, tiled=True).T
-
-        down = lax.psum_scatter(
-            wide[: 4 * width].reshape(4, width, width), "dp", scatter_dimension=1, tiled=True
-        )
-        down = down.transpose(0, 2, 1).reshape(4 * width, share)
-        up = scattered(UP, 4)
-        out = scattered(OUT, 1)
-        qkv = scattered(QKV, 3)
+    token = lax.psum(small[12], ("dp", "section"))
+    vectors = lax.psum(small[:12], "dp")
+    wide = grads.astype(F32) * scale
+
+    def scattered(first, count):
+        part = wide[first * width : (first + count) * width]
+        return lax.psum_scatter(part, "dp", scatter_dimension=0, tiled=True).T
+
+    down = lax.psum_scatter(
+        wide[: 4 * width].reshape(4, width, width), "dp", scatter_dimension=1, tiled=True
+    )
+    down = down.transpose(0, 2, 1).reshape(4 * width, share)
+    up = scattered(UP, 4)
+    out = scattered(OUT, 1)
+    qkv = scattered(QKV, 3)
 
     def cut(first, count):
         return lax.dynamic_slice(vectors, (first, me * share), (count, share))
 
     up_vector = lax.dynamic_slice(vectors[7:11].reshape(-1), (me * 4 * share,), (4 * share,))
-    return (
-        boundary,
-        token,
-        cut(0, 2)[None],
-        cut(2, 2)[None],
-        qkv[None],
-        cut(4, 2)[None],
-        out[None],
-        cut(6, 1),
-        up[None],
-        up_vector[None],
-        down[None],
-        cut(11, 1),
-    )
+    parts = (bound.transpose(2, 0, 1, 3), token, cut(0, 2)[None], cut(2, 2)[None], qkv[None])
+    parts += (cut(4, 2)[None], out[None], cut(6, 1), up[None], up_vector[None], down[None], cut(11, 1))
+    return parts
 
 
 def solution(mesh):

time: 253 us -> 191 us (0.75)
  Pallas kernels: 234 us -> 189 us
  local copies, waits for them, and re-layouts: 17 us -> 0 us
    pallas_call x1 -> x2, Pallas kernels: 234 us -> 189 us  [the longest x1 186 us: on_device(): pl.pallas_call(functools.partial(kernel, geo), out_shape=out_shape, in_sp...]
    broadcast_in_dim x4 -> x0, local copies, waits for them, and re-layouts: 4.42 us -> none  [the longest x1 1.58 us: on_device(): out[None]]
    slice x3 -> x0, local copies, waits for them, and re-layouts: 3.95 us -> none  [the longest x1 1.8 us: on_device(): qkv = grads[9:].transpose(2, 0, 1).reshape(width, 3 * share)]
    unnamed x3 -> x0, local copies, waits for them, and re-layouts: 3.08 us -> none
where the time goes in v2:
time: 191 us; the launch traced here: 190 us
  Pallas kernels  189 us (99%)
    pallas_call x1, Pallas kernels, on_device(): pl.pallas_call(functools.partial(kernel, geo), out_shape=out_shape, in_sp...  186 us

profile of v2, /device:TPU:0, one launch (start us, length us, event | category | flops | bytes accessed | tf_op | source)
XLA Modules:
  0.0 190.2 jit_solution(2083593933297931518)
XLA Ops:
  0.6 185.9 %relay.1 = (f32[3,196,1,768]{3,2,1,0:T(1,128)}, f32[48,3072]{1,0:T(8,128)}, f32[192,768]{1,0:T(8,128)}, f32[48,768]{1,0:T(8,128)}, f32[144,768]{1,0:T(8,128)}, /...) custom-call(bf16[3,196,768]{2,1,0:T(8,128)(2,1)} %refs_0_.1, ...), custom_call_target="tpu_custom_call" | custom-call | flops 26499612672 | bytes 28311552 | tf_op jit(solution)/shard_map/relay/pallas_call | solution.py:836
  186.5 3.5 %hand_on.1 = (f32[3,196,1,768]{3,2,1,0:T(1,128)}, f32[48,3072]{1,0:T(8,128)}, f32[192,768]{1,0:T(8,128)}, f32[48,768]{1,0:T(8,128)}, f32[144,768]{1,0:T(8,128)},...) custom-call(f32[3,196,1,768]{3,2,1,0:T(1,128)} %get-tuple-element.36, ...), custom_call_target="tpu_custom_call" | custom-call | tf_op jit(solution)/shard_map/hand_on/pallas_call | solution.py:867

commit v3 on v2

--- a/solution.py
+++ b/solution.py
@@ -12,8 +12,8 @@
 EPS = 1e-06
 BF = jnp.bfloat16
 F32 = jnp.float32
-Z_FIRST = (2, 4)
-WINDOW = 2
+Z_FIRST = (3, 5)
+WINDOW = 4
 UNITS = 12
 UP, OUT, QKV, DOWN_W = 4, 8, 9, 12
 SMALL = 16
@@ -90,13 +90,12 @@
     def _():
         pltpu.make_async_copy(r["cotangent"], r["pin"], r["pin_sem"]).start()
 
-    for index in range(UNITS):
+    for index in range(3):
         weight_copy(index).start()
 
     barrier = pltpu.get_barrier_semaphore()
     for partner in partners:
         pl.semaphore_signal(barrier, inc=1, device_id=partner)
-    pl.semaphore_wait(barrier, len(partners))
 
     r["sm"][...] = jnp.zeros_like(r["sm"])
     pltpu.make_async_copy(r["patches"], r["pin"], r["pin_sem"]).wait()
@@ -155,7 +154,7 @@
 
     def attention_forward(img, pair):
         rows = image_rows(img)
-        lanes = pl.ds(pl.multiple_of(128 * pair, 128), 128)
+        lanes = pl.ds(128 * pair, 128)
         queries = r["qkv"][0, rows, lanes]
         keys = r["qkv"][1, rows, lanes]
         values = r["qkv"][2, rows, lanes]
@@ -172,11 +171,13 @@
         lane = lax.broadcasted_iota(jnp.int32, mixed[0].shape, 1)
         r["o"][rows, lanes] = jnp.where(lane < width // HEADS, mixed[0], mixed[1]).astype(BF)
 
-    def wait_weights(step, indices):
+    def wait_weights(step, indices, then_start=()):
         @pl.when(step == 0)
         def _():
             for index in indices:
                 weight_copy(index).wait()
+            for index in then_start:
+                weight_copy(index).start()
 
     def forward(step, img):
         rows = image_rows(img)
@@ -201,7 +202,7 @@
             forward_send(img).wait_recv()
 
         norm_forward(img, lambda b, at: r["x"][at, :].astype(F32), 0, r["n1"], r["a1"])
-        wait_weights(step, range(0, 3))
+        wait_weights(step, range(0, 3), range(3, UNITS))
         for j in range(3):
             projected = dot(r["a1"][rows, :], wg[unit_rows(QKV + j), :], 1, 0)
             if j == 0:
@@ -210,19 +211,16 @@
                 projected = projected + r["qv_bias"][1:2, :]
             r["qkv"][j, rows, :] = projected.astype(BF)
 
-        def three_pairs(half, carry):
-            for pair in range(HEADS // 4):
-                attention_forward(img, half * (HEADS // 4) + pair)
-            return carry
-
-        lax.fori_loop(0, 2, three_pairs, 0)
-        wait_weights(step, range(3, UNITS))
+        for pair in range(HEADS // 2):
+            attention_forward(img, pair)
+        wait_weights(step, range(3, 4))
         r["yb"][...] = (
             r["x"][rows, :].astype(F32)
             + dot(r["o"][rows, :], wg[unit_rows(OUT), :], 1, 0)
             + r["out_bias"][...]
         )
         norm_forward(img, lambda b, at: r["yb"][16 * b : 16 * (b + 1), :], 1, r["n2"], r["a2"])
+        wait_weights(step, range(4, UNITS))
         result = None
         for j in range(4):
             hidden = dot(r["a2"][rows, :], wg[unit_rows(UP + j), :], 1, 0)
@@ -236,6 +234,10 @@
             result = term if result is None else result + term
         result = r["yb"][...] + result + r["down_bias"][...]
 
+        @pl.when(step == 0)
+        def _():
+            pl.semaphore_wait(barrier, len(partners))
+
         @pl.when(first)
         def _():
             r["send"][rows, :] = result.astype(BF)
@@ -258,6 +260,7 @@
             r["dy"][image_rows(img, 0, seq), :] = r["pin"][img]
 
     def norm_backward(img, which, gradient, incoming):
+        results = []
         gain = r["gains"][which : which + 1, :]
         normed = r["n1"] if which == 0 else r["n2"]
         gain_sum = jnp.zeros((8, width), F32)
@@ -271,9 +274,10 @@
             mean = jnp.mean(scaled, axis=1, keepdims=True)
             along = jnp.mean(scaled * unit, axis=1, keepdims=True)
             local = (scaled - mean - unit * along) * r["cols"][rows, which : which + 1]
-            yield b, rows, local + incoming(b, rows)
+            results.append((b, rows, local + incoming(b, rows)))
         r["sm"][which : which + 1, :] += jnp.sum(gain_sum, axis=0, keepdims=True)
         r["sm"][2 + which : 3 + which, :] += jnp.sum(shift_sum, axis=0, keepdims=True)
+        return results
 
     def backward_mlp(img):
         rows = image_rows(img)
@@ -300,7 +304,7 @@
 
     def attention_backward(img, pairs):
         rows = image_rows(img)
-        places = [pl.ds(pl.multiple_of(128 * pair, 128), 128) for pair in pairs]
+        places = [pl.ds(128 * pair, 128) for pair in pairs]
         loaded = []
         for pair, lanes in zip(pairs, places):
             probs = [r["prob"][img * HEADS + 2 * pair + head] for head in range(2)]
@@ -333,11 +337,7 @@
         rows = image_rows(img)
         r["do"][...] = dot(r["n2"][rows, :], wg[unit_rows(OUT), :], 1, 1).astype(BF)
 
-        def three_pairs(half, carry):
-            attention_backward(img, [half * (HEADS // 4) + pair for pair in range(HEADS // 4)])
-            return carry
-
-        lax.fori_loop(0, 2, three_pairs, 0)
+        attention_backward(img, range(HEADS // 2))
         back = None
         for j in range(3):
             term = dot(r["qkv"][j, rows, :], wg[unit_rows(QKV + j), :], 1, 1)
@@ -530,6 +530,9 @@
                     at = 8 * half + b
                 if reduce_here:
                     owner, part = at // spread, lax.rem(at, spread)
+                    if spread == 4:
+                        part = b % spread
+                        z_first = UP + part < Z_FIRST[1]
                     rows = unit_rows(first_unit + part, place(owner, z_first) * block, block)
                 else:
                     rows = unit_rows(first_unit, at * block, block)
@@ -546,37 +549,24 @@
                 )
                 if reduce_here:
                     core_copy(j).start()
-
-                    @pl.when(j > 0)
-                    def _():
-                        if z_first:
-                            pl.when(j == Z_FIRST[0])(lambda: add_core(j - 1, False))
-                            pl.when(j > Z_FIRST[0])(lambda: add_core(j - 1, True))
-                        else:
-                            add_core(j - 1, False)
-
+                    pl.when(j > 0)(lambda: add_core(j - 1, False))
                 return carry
 
             return body
 
         lax.fori_loop(0, Z_FIRST[0], one(False), 0)
-        lax.fori_loop(*Z_FIRST, one(True), 0)
+        lax.fori_loop(Z_FIRST[0], 4, one(True), 0)
         if reduce_here:
-            add_core(Z_FIRST[1] - 1, True)
+            add_core(3, True)
 
     def start_units(begin, end):
         if reduce_here:
             for unit in range(begin, end):
                 core_copy(unit).start()
 
-    def z_first_hops(hop):
+    def add_y_if(when, unit):
         if reduce_here:
-
-            def one(unit, carry):
-                z_hop(hop, unit, True)
-                return carry
-
-            lax.fori_loop(*Z_FIRST, one, 0)
+            pl.when(when)(lambda: add_y(unit))
 
     def turn(step, carry):
         img = lax.rem(step, images)
@@ -600,9 +590,7 @@
         def _():
             backward_mlp(img)
 
-        @pl.when(down_now & first)
-        def _():
-            z_first_hops(1)
+        add_y_if(down_now & first, 0)
 
         @pl.when(back_now)
         def _():
@@ -619,14 +607,11 @@
     lax.fori_loop(0, 4, up_one, 0)
     start_units(UP, OUT)
     if reduce_here:
-        for unit in range(UP, UP + WINDOW):
+        add_core(UP, True)
+        for unit in range(Z_FIRST[1], OUT):
             add_core(unit, False)
-
-    @pl.when(second)
-    def _():
-        z_first_hops(1)
-
-    z_first_hops(2)
+    add_y_if(first, 1)
+    add_y_if(second, 0)
     weight_gradient(lambda half: r["n2"][:, half_lanes(half)], r["o"][...], 0, OUT, 1)
     start_units(OUT, QKV)
 
@@ -636,7 +621,6 @@
 
     lax.fori_loop(0, 3, qkv_one, 0)
     start_units(QKV, UNITS)
-    z_first_hops(3)
 
     for img in range(images):
         bound_copy(img).start()
@@ -682,13 +666,19 @@
             r["g_token"][...] = token.reshape(width)
 
         def drain(k, carry):
-            @pl.when(k < in_order)
+            @pl.when((k < in_order) & ((k > 1) | second))
             def _():
                 add_y(unit_at(k))
 
-            @pl.when((k >= Z_FIRST[0]) & (k + WINDOW < in_order))
+            @pl.when((k > 1) & (k + WINDOW < in_order))
             def _():
                 add_core(unit_at(k + WINDOW), False)
+
+            for hop in (1, 2, 3):
+
+                @pl.when((k >= hop) & (k < hop + Z_FIRST[1] - Z_FIRST[0]))
+                def _(hop=hop):
+                    z_hop(hop, Z_FIRST[0] + k - hop, True)
 
             for hop in (1, 2, 3):
 
@@ -702,14 +692,13 @@
                 def _(t=t):
                     small_step(t)
 
-            @pl.when(k == 2)
+            @pl.when((k >= 5) & (k < 5 + Z_FIRST[1] - Z_FIRST[0]))
             def _():
-                for unit in range(*Z_FIRST):
-                    finish_z_first(unit)
+                finish_z_first(Z_FIRST[0] + k - 5)
 
             return carry
 
-        lax.fori_loop(0, in_order + 3, drain, 0)
+        lax.fori_loop(1, in_order + 3, drain, 0)
 
         def sent(z_first):
             def body(unit, carry):

time: 191 us -> 170 us (0.89)
  Pallas kernels: 189 us -> 169 us
    pallas_call x1, Pallas kernels: 186 us -> 165 us  [on_device(): pl.pallas_call(functools.partial(kernel, geo), out_shape=out_shape, in_sp...]
where the time goes in v3:
time: 170 us
  Pallas kernels  169 us (99%)
    pallas_call x1, Pallas kernels, on_device(): pl.pallas_call(functools.partial(kernel, geo), out_shape=out_shape, in_sp...  165 us
    pallas_call x1, Pallas kernels, on_device(): pl.pallas_call(functools.partial(hand_on, count), out_shape=out_shape, in...  3.52 us

profile of v3, /device:TPU:0, one launch (start us, length us, event | category | flops | bytes accessed | tf_op | source)
XLA Modules:
  0.0 169.5 jit_solution(10631104750465906135)
XLA Ops:
  0.6 165.2 %relay.1 = (f32[3,196,1,768]{3,2,1,0:T(1,128)}, f32[48,3072]{1,0:T(8,128)}, f32[192,768]{1,0:T(8,128)}, f32[48,768]{1,0:T(8,128)}, f32[144,768]{1,0:T(8,128)}, /...) custom-call(bf16[3,196,768]{2,1,0:T(8,128)(2,1)} %refs_0_.1, ...), custom_call_target="tpu_custom_call" | custom-call | flops 26499612672 | bytes 28311552 | tf_op jit(solution)/shard_map/relay/pallas_call | solution.py:825
  165.8 3.5 %hand_on.1 = (f32[3,196,1,768]{3,2,1,0:T(1,128)}, f32[48,3072]{1,0:T(8,128)}, f32[192,768]{1,0:T(8,128)}, f32[48,768]{1,0:T(8,128)}, f32[144,768]{1,0:T(8,128)},...) custom-call(f32[3,196,1,768]{3,2,1,0:T(1,128)} %get-tuple-element.36, ...), custom_call_target="tpu_custom_call" | custom-call | tf_op jit(solution)/shard_map/hand_on/pallas_call | solution.py:856

commit v4 on v3

--- a/solution.py
+++ b/solution.py
@@ -12,11 +12,13 @@
 EPS = 1e-06
 BF = jnp.bfloat16
 F32 = jnp.float32
-Z_FIRST = (3, 5)
+Z_FIRST = 2
 WINDOW = 4
+LAG = (0, 1, 2, 3)
 UNITS = 12
 UP, OUT, QKV, DOWN_W = 4, 8, 9, 12
 SMALL = 16
+SMALL_AT = (1, 7, 9, 10, 11)
 INV_SQRT2 = 1.0 / math.sqrt(2.0)
 INV_SQRT2PI = 1.0 / math.sqrt(2.0 * math.pi)
 
@@ -39,16 +41,12 @@
     block = width // 16
     names = ["patches", "cotangent", "mask", "token", "gains", "shifts", "qv_bias", "out_bias", "up_bias"]
     names += ["down_bias", "w_qkv", "w_out", "w_up", "w_down", "bound"]
-    if reduce_here:
-        names += ["down", "up", "out", "three", "g_gains", "g_shifts", "g_qv", "g_out", "g_up", "g_down"]
-        names += ["g_token"]
-    else:
-        names += ["grads", "small"]
+    names += ["grads", "small"]
     names += ["wg", "x", "n1", "a1", "qkv", "o", "n2", "a2", "act", "gp", "dy", "send", "prob", "cols"]
     names += ["yb", "da", "tb", "do", "pin", "plain", "sm", "sms", "smr"]
     names += ["pin_sem", "w_sem", "out_sem", "fs", "fr", "bs", "br"]
     if reduce_here:
-        names += ["rc", "ry", "zb", "zf", "cs", "cr", "ys", "yr", "rs", "rr", "ls", "lr", "ss", "sr"]
+        names += ["stage", "rc", "ry", "zb", "zf", "cs", "cr", "ys", "yr", "rs", "rr", "ls", "lr", "ss", "sr", "put_sem"]
     r = dict(zip(names, refs, strict=True))
     wg = r["wg"]
     me = lax.axis_index("dp")
@@ -82,23 +80,35 @@
         unit, source = weight_copies[index]
         return pltpu.make_async_copy(source, wg.at[unit_rows(unit), :], r["w_sem"].at[index])
 
+    def own_copy(source, img):
+        return pltpu.make_async_copy(r[source].at[img], r["pin"].at[img], r["pin_sem"].at[img])
+
     @pl.when(first)
     def _():
-        pltpu.make_async_copy(r["patches"], r["pin"], r["pin_sem"]).start()
+        own_copy("patches", 0).start()
 
     @pl.when(second)
     def _():
-        pltpu.make_async_copy(r["cotangent"], r["pin"], r["pin_sem"]).start()
+        own_copy("cotangent", 0).start()
 
     for index in range(3):
         weight_copy(index).start()
+
+    @pl.when(first)
+    def _():
+        for img in range(1, images):
+            own_copy("patches", img).start()
+
+    @pl.when(second)
+    def _():
+        for img in range(1, images):
+            own_copy("cotangent", img).start()
 
     barrier = pltpu.get_barrier_semaphore()
     for partner in partners:
         pl.semaphore_signal(barrier, inc=1, device_id=partner)
 
     r["sm"][...] = jnp.zeros_like(r["sm"])
-    pltpu.make_async_copy(r["patches"], r["pin"], r["pin_sem"]).wait()
 
     def image_rows(img, offset=0, size=pad):
         return pl.ds(pl.multiple_of(img * pad + offset, 16), size)
@@ -179,30 +189,12 @@
             for index in then_start:
                 weight_copy(index).start()
 
-    def forward(step, img):
+    def forward_stages(img, step=None):
         rows = image_rows(img)
-
-        @pl.when(first)
-        def _():
-            tail = image_rows(img, seq // 16 * 16, 16)
-            r["x"][tail, :] = jnp.zeros((16, width), BF)
-            row = r["mask"][pl.ds(img, 1), :]
-            at_row = lax.broadcasted_iota(jnp.int32, (pad, seq), 0)
-            at_lane = lax.broadcasted_iota(jnp.int32, (pad, seq), 1)
-            covered = jnp.where((at_row == at_lane) & (row == 1), 1.0, 0.0)
-            column = jnp.sum(covered, axis=1, keepdims=True)
-            r["cols"][rows, 2:3] = column
-            token = r["token"][...][None, :].astype(F32)
-            kept = r["pin"][img].astype(F32)
-            mixed = jnp.where(column[:seq] > 0.5, token, kept)
-            r["x"][image_rows(img, 0, seq), :] = mixed.astype(BF)
-
-        @pl.when(second)
-        def _():
-            forward_send(img).wait_recv()
-
         norm_forward(img, lambda b, at: r["x"][at, :].astype(F32), 0, r["n1"], r["a1"])
-        wait_weights(step, range(0, 3), range(3, UNITS))
+        yield
+        if step is not None:
+            wait_weights(step, range(0, 3), range(3, UNITS))
         for j in range(3):
             projected = dot(r["a1"][rows, :], wg[unit_rows(QKV + j), :], 1, 0)
             if j == 0:
@@ -210,17 +202,22 @@
             if j == 2:
                 projected = projected + r["qv_bias"][1:2, :]
             r["qkv"][j, rows, :] = projected.astype(BF)
-
+            yield
         for pair in range(HEADS // 2):
             attention_forward(img, pair)
-        wait_weights(step, range(3, 4))
+            yield
+        if step is not None:
+            wait_weights(step, range(3, 4))
         r["yb"][...] = (
             r["x"][rows, :].astype(F32)
             + dot(r["o"][rows, :], wg[unit_rows(OUT), :], 1, 0)
             + r["out_bias"][...]
         )
+        yield
         norm_forward(img, lambda b, at: r["yb"][16 * b : 16 * (b + 1), :], 1, r["n2"], r["a2"])
-        wait_weights(step, range(4, UNITS))
+        yield
+        if step is not None:
+            wait_weights(step, range(4, UNITS))
         result = None
         for j in range(4):
             hidden = dot(r["a2"][rows, :], wg[unit_rows(UP + j), :], 1, 0)
@@ -232,7 +229,44 @@
             r["gp"][j, rows, :] = slope.astype(BF)
             term = dot(active, wg[unit_rows(DOWN_W + j), :], 1, 0)
             result = term if result is None else result + term
-        result = r["yb"][...] + result + r["down_bias"][...]
+            yield
+        yield r["yb"][...] + result + r["down_bias"][...]
+
+    def keep_result(img, result):
+        for at in range(0, seq, 16):
+            write_bound(img, at, result[at : at + 16])
+
+    def forward(step, img):
+        @pl.when(first)
+        def _():
+            tail = image_rows(img, seq // 16 * 16, 16)
+            r["x"][tail, :] = jnp.zeros((16, width), BF)
+            own_copy("patches", img).wait()
+            row = r["mask"][pl.ds(img, 1), :]
+            at_row = lax.broadcasted_iota(jnp.int32, (pad, seq), 0)
+            at_lane = lax.broadcasted_iota(jnp.int32, (pad, seq), 1)
+            covered = jnp.where((at_row == at_lane) & (row == 1), 1.0, 0.0)
+            column = jnp.sum(covered, axis=1, keepdims=True)
+            r["cols"][image_rows(img), 2:3] = column
+            token = r["token"][...][None, :].astype(F32)
+            kept = r["pin"][img].astype(F32)
+            mixed = jnp.where(column[:seq] > 0.5, token, kept)
+            r["x"][image_rows(img, 0, seq), :] = mixed.astype(BF)
+
+        @pl.when(second & (step == 0))
+        def _():
+            for at in range(images):
+                own_copy("cotangent", at).wait()
+                tail = at * pad + seq // 16 * 16
+                r["dy"][tail : tail + 16, :] = jnp.zeros((16, width), BF)
+                r["dy"][at * pad : at * pad + seq, :] = r["pin"][at]
+
+        @pl.when(second)
+        def _():
+            forward_send(img).wait_recv()
+
+        for result in forward_stages(img, step):
+            pass
 
         @pl.when(step == 0)
         def _():
@@ -240,24 +274,12 @@
 
         @pl.when(first)
         def _():
-            r["send"][rows, :] = result.astype(BF)
+            r["send"][image_rows(img), :] = result.astype(BF)
             forward_send(img).start()
 
         @pl.when(second)
         def _():
-            for at in range(0, seq, 16):
-                write_bound(img, at, result[at : at + 16])
-
-    def take_gradient(img):
-        @pl.when(first)
-        def _():
-            backward_send(img).wait_recv()
-
-        @pl.when(second)
-        def _():
-            tail = image_rows(img, seq // 16 * 16, 16)
-            r["dy"][tail, :] = jnp.zeros((16, width), BF)
-            r["dy"][image_rows(img, 0, seq), :] = r["pin"][img]
+            keep_result(img, result)
 
     def norm_backward(img, which, gradient, incoming):
         results = []
@@ -279,7 +301,7 @@
         r["sm"][2 + which : 3 + which, :] += jnp.sum(shift_sum, axis=0, keepdims=True)
         return results
 
-    def backward_mlp(img):
+    def backward_mlp_stages(img):
         rows = image_rows(img)
         incoming = r["dy"][rows, :]
         r["sm"][11:12, :] += jnp.sum(incoming.astype(F32), axis=0, keepdims=True)
@@ -292,6 +314,7 @@
             r["gp"][j, rows, :] = narrow
             term = dot(narrow, wg[unit_rows(UP + j), :], 1, 1)
             back = term if back is None else back + term
+            yield
         r["tb"][...] = back
         bias_sum = jnp.zeros((8, width), F32)
         for b, block_rows, middle in norm_backward(
@@ -301,8 +324,9 @@
             r["da"][16 * b : 16 * (b + 1), :] = middle
             r["n2"][block_rows, :] = middle.astype(BF)
         r["sm"][6:7, :] += jnp.sum(bias_sum, axis=0, keepdims=True)
-
-    def attention_backward(img, pairs):
+        yield
+
+    def attention_backward_stages(img, pairs):
         rows = image_rows(img)
         places = [pl.ds(128 * pair, 128) for pair in pairs]
         loaded = []
@@ -326,6 +350,7 @@
                 total = terms if total is None else [a + b for a, b in zip(total, terms)]
             d_query, d_key, d_value = total
             results.append((d_query * (1.0 / math.sqrt(width // HEADS)), d_key, d_value))
+            yield
         for (d_query, d_key, d_value), lanes in zip(results, places):
             r["sm"][4:5, lanes] += jnp.sum(d_query, axis=0, keepdims=True)
             r["sm"][5:6, lanes] += jnp.sum(d_value, axis=0, keepdims=True)
@@ -333,20 +358,34 @@
             r["qkv"][1, rows, lanes] = d_key.astype(BF)
             r["qkv"][2, rows, lanes] = d_value.astype(BF)
 
-    def backward_attention(img):
+    def backward_attention_stages(img):
         rows = image_rows(img)
         r["do"][...] = dot(r["n2"][rows, :], wg[unit_rows(OUT), :], 1, 1).astype(BF)
-
-        attention_backward(img, range(HEADS // 2))
+        yield
+        yield from attention_backward_stages(img, range(HEADS // 2))
+        yield
         back = None
         for j in range(3):
             term = dot(r["qkv"][j, rows, :], wg[unit_rows(QKV + j), :], 1, 1)
             back = term if back is None else back + term
+            yield
         r["tb"][...] = back
         for b, block_rows, entry in norm_backward(
             img, 0, r["tb"], lambda b, block_rows: r["da"][16 * b : 16 * (b + 1), :]
         ):
             r["da"][16 * b : 16 * (b + 1), :] = entry
+        yield
+
+    def send_back(img):
+        r["send"][image_rows(img), :] = r["da"][...].astype(BF)
+        backward_send(img).start()
+
+    def run(stages):
+        for _ in stages:
+            pass
+
+    def backward_attention(img):
+        run(backward_attention_stages(img))
 
         @pl.when(first)
         def _():
@@ -361,8 +400,7 @@
 
         @pl.when(second)
         def _():
-            r["send"][rows, :] = r["da"][...].astype(BF)
-            backward_send(img).start()
+            send_back(img)
 
     half_rows, quarter = width // 2, width // 4
     across_core, across_y = dp_at(1), dp_at(2)
@@ -376,36 +414,45 @@
             device_id=across_core,
         )
 
+    in_order = UNITS - Z_FIRST
+
     def y_slot(unit, z_first):
         if z_first:
-            at = (UNITS - Z_FIRST[1] + Z_FIRST[0]) * quarter + (unit - Z_FIRST[0]) * block
+            at = in_order * quarter + unit // 4 * block
             return r["ry"].at[pl.ds(pl.multiple_of(at, 16), block), :]
         return r["ry"].at[pl.ds(pl.multiple_of(index_of(unit) * quarter, 16), quarter), :]
 
     def index_of(unit):
-        return jnp.where(unit < Z_FIRST[0], unit, unit - (Z_FIRST[1] - Z_FIRST[0]))
-
-    def y_copy(unit, z_first):
+        return unit - 1 - jnp.minimum(unit // 4, Z_FIRST - 1)
+
+    def unit_at(index):
+        return index + 1 + jnp.minimum(index // 3, Z_FIRST - 1)
+
+    def y_copy(unit, z_first, part=0):
+        landing = y_slot(unit, z_first)
         if z_first:
             size, away = block, half_rows * core + 2 * block * z_at + block * (1 - y_at)
         else:
-            size, away = quarter, half_rows * core + quarter * (1 - y_at)
+            size = 2 * block
+            away = half_rows * core + quarter * (1 - y_at) + size * part
+            landing = landing.at[pl.ds(size * part, size), :]
         return pltpu.make_async_remote_copy(
             src_ref=wg.at[unit_rows(unit, away, size), :],
-            dst_ref=y_slot(unit, z_first),
-            send_sem=r["ys"].at[unit],
-            recv_sem=r["yr"].at[unit],
+            dst_ref=landing,
+            send_sem=r["ys"].at[2 * unit + part],
+            recv_sem=r["yr"].at[2 * unit + part],
             device_id=across_y,
         )
 
     def z_rows(unit, owner, z_first):
         if z_first:
             return unit_rows(unit, half_rows * core + 2 * block * owner, 2 * block)
-        return unit_rows(unit, half_rows * core + quarter * y_at + block * owner, block)
+        at = (0, 2, 3, 1)[owner]
+        return unit_rows(unit, half_rows * core + quarter * y_at + block * at, block)
 
     def z_slot(unit, slot, z_first):
         if z_first:
-            at = (unit - Z_FIRST[0]) * 10 * block + slot * 2 * block
+            at = unit // 4 * 10 * block + slot * 2 * block
             return r["zf"].at[pl.ds(pl.multiple_of(at, 16), 2 * block), :]
         at = index_of(unit) * 5 * block + slot * block
         return r["zb"].at[pl.ds(pl.multiple_of(at, 16), block), :]
@@ -434,17 +481,18 @@
         if z_first:
             z_start(unit, True)
         else:
-            y_copy(unit, False).start()
-
-    def z_start(unit, z_first):
+            for part in range(2):
+                y_copy(unit, False, part).start()
+
+    def z_start(unit, z_first, from_bottom=(3, 2, 1), from_top=(0, 1, 2)):
         @pl.when(z_at == 0)
         def _():
-            for owner in (3, 2, 1):
+            for owner in from_bottom:
                 z_copy(unit, owner, 1, z_first, 1).start()
 
         @pl.when(z_at == 3)
         def _():
-            for owner in (0, 1, 2):
+            for owner in from_top:
                 z_copy(unit, owner, -1, z_first, 2).start()
 
     def z_hop(hop, unit, z_first):
@@ -467,7 +515,6 @@
                 total = total + z_slot(unit, 4, z_first)[...].astype(F32)
             if z_first:
                 wg[z_rows(unit, here, True), :] = total.astype(BF)
-                y_copy(unit, True).start()
             else:
                 put(unit, total)
 
@@ -485,24 +532,12 @@
             if hop >= 2:
                 finish(3 - hop)
 
+    def put_copy(unit):
+        return pltpu.make_async_copy(r["stage"].at[unit], r["grads"].at[unit], r["put_sem"].at[unit])
+
     def put(unit, total):
-        total = total * scale
-
-        @pl.when(unit < UP)
-        def _():
-            r["down"][:, pl.ds(pl.multiple_of(jnp.minimum(unit, 3) * width, 128), width)] = total
-
-        @pl.when((unit >= UP) & (unit < OUT))
-        def _():
-            r["up"][pl.ds(pl.multiple_of(jnp.clip(unit - UP, 0, 3) * block, 16), block), :] = total
-
-        @pl.when(unit == OUT)
-        def _():
-            r["out"][...] = total
-
-        @pl.when(unit >= QKV)
-        def _():
-            r["three"][pl.ds(pl.multiple_of(jnp.clip(unit - QKV, 0, 2) * block, 16), block), :] = total
+        r["stage"][unit] = total * scale
+        put_copy(unit).start()
 
     def finish_z_first(unit):
         y_copy(unit, True).wait_recv()
@@ -511,15 +546,21 @@
         put(unit, wg[mine, :].astype(F32) + came.astype(F32))
 
     def add_y(unit):
-        y_copy(unit, False).wait_recv()
-        add_rows(unit, half_rows * core + quarter * y_at, y_slot(unit, False), quarter)
-        z_start(unit, False)
+        size = 2 * block
+        for part in range(2):
+            y_copy(unit, False, part).wait_recv()
+            came = y_slot(unit, False).at[pl.ds(size * part, size), :]
+            add_rows(unit, half_rows * core + quarter * y_at + size * part, came, size)
+            if part == 0:
+                z_start(unit, False, (3,), (0,))
+            else:
+                z_start(unit, False, (2, 1), (1, 2))
 
     def place(owner, z_first):
         core_of, y_of, z_of = lax.rem(owner, 2), lax.rem(owner // 2, 2), owner // 4
         if z_first:
             return core_of * 8 + z_of * 2 + y_of
-        return core_of * 8 + y_of * 4 + z_of
+        return core_of * 8 + y_of * 4 + jnp.where(z_of == 0, 0, jnp.where(z_of == 3, 1, z_of + 1))
 
     def weight_gradient(left, right, chunk, first_unit, spread, z_first=False):
         for half in range(2):
@@ -532,7 +573,7 @@
                     owner, part = at // spread, lax.rem(at, spread)
                     if spread == 4:
                         part = b % spread
-                        z_first = UP + part < Z_FIRST[1]
+                        z_first = part == 0
                     rows = unit_rows(first_unit + part, place(owner, z_first) * block, block)
                 else:
                     rows = unit_rows(first_unit, at * block, block)
@@ -549,15 +590,17 @@
                 )
                 if reduce_here:
                     core_copy(j).start()
-                    pl.when(j > 0)(lambda: add_core(j - 1, False))
+                    if not z_first:
+                        pl.when(j == 1)(lambda: add_core(0, True))
+                        pl.when(j > 1)(lambda: add_core(j - 1, False))
                 return carry
 
             return body
 
-        lax.fori_loop(0, Z_FIRST[0], one(False), 0)
-        lax.fori_loop(Z_FIRST[0], 4, one(True), 0)
+        lax.fori_loop(0, 1, one(True), 0)
+        lax.fori_loop(1, 4, one(False), 0)
         if reduce_here:
-            add_core(3, True)
+            add_core(3, False)
 
     def start_units(begin, end):
         if reduce_here:
@@ -578,19 +621,17 @@
         def _():
             forward(step, img)
 
+        @pl.when(back_now & first)
+        def _():
+            backward_send(img).wait_recv()
+
+        @pl.when(down_now)
+        def _():
+            down_gradient()
+
         @pl.when(back_now)
         def _():
-            take_gradient(img)
-
-        @pl.when(down_now)
-        def _():
-            down_gradient()
-
-        @pl.when(back_now)
-        def _():
-            backward_mlp(img)
-
-        add_y_if(down_now & first, 0)
+            run(backward_mlp_stages(img))
 
         @pl.when(back_now)
         def _():
@@ -604,15 +645,16 @@
         weight_gradient(lambda half: r["gp"][c, :, half_lanes(half)], r["a2"][...], c, UP, 4)
         return carry
 
+    add_y_if(first, 1)
     lax.fori_loop(0, 4, up_one, 0)
     start_units(UP, OUT)
     if reduce_here:
         add_core(UP, True)
-        for unit in range(Z_FIRST[1], OUT):
+        for unit in range(UP + 1, OUT):
             add_core(unit, False)
-    add_y_if(first, 1)
-    add_y_if(second, 0)
-    weight_gradient(lambda half: r["n2"][:, half_lanes(half)], r["o"][...], 0, OUT, 1)
+    add_y_if(first, 2)
+    add_y_if(second, 1)
+    weight_gradient(lambda half: r["n2"][:, half_lanes(half)], r["o"][...], 0, OUT, 1, Z_FIRST == 3)
     start_units(OUT, QKV)
 
     def qkv_one(c, carry):
@@ -621,9 +663,23 @@
 
     lax.fori_loop(0, 3, qkv_one, 0)
     start_units(QKV, UNITS)
+    if reduce_here and Z_FIRST == 3:
+        add_core(OUT, True)
 
     for img in range(images):
         bound_copy(img).start()
+
+    def finish_images():
+        for img in range(images):
+            bound_copy(img).wait()
+
+            @pl.when(first)
+            def _(img=img):
+                forward_send(img).wait_send()
+
+            @pl.when(second)
+            def _(img=img):
+                backward_send(img).wait_send()
 
     if reduce_here:
         hops = [dp_at(1), dp_at(2), dp_at(8), dp_at(4), across]
@@ -639,10 +695,6 @@
 
         r["sms"][0] = r["sm"][...]
         small_send(0).start()
-        in_order = UNITS - (Z_FIRST[1] - Z_FIRST[0])
-
-        def unit_at(index):
-            return jnp.where(index < Z_FIRST[0], index, index + Z_FIRST[1] - Z_FIRST[0])
 
         def small_step(t):
             small_send(t).wait_recv()
@@ -652,18 +704,28 @@
                 return
             total = r["sms"][4] * scale
             shift = lax.rem(width - block * me, width)
-            turned = pltpu.roll(total, shift, 1)[:, :block]
-            r["g_gains"][0] = turned[0:2]
-            r["g_shifts"][0] = turned[2:4]
-            r["g_qv"][0] = turned[4:6]
-            r["g_out"][...] = turned[6:7]
-            r["g_down"][...] = turned[11:12]
+            r["small"][...] = pltpu.roll(total, shift, 1)
+            r["small"][12:13, :] = (r["sms"][4, 12:13, :] + r["smr"][4, 12:13, :]) * scale
             up_row = r["sms"][4, pl.ds(7 + me // 4, 1), :] * scale
             up_shift = lax.rem(width - 4 * block * lax.rem(me, 4), width)
             spread_row = jnp.broadcast_to(up_row, (8, width))
-            r["g_up"][...] = pltpu.roll(spread_row, up_shift, 1)[0:1, : 4 * block]
-            token = (r["sms"][4, 12:13, :] + r["smr"][4, 12:13, :]) * scale
-            r["g_token"][...] = token.reshape(width)
+            r["small"][13:14, :] = pltpu.roll(spread_row, up_shift, 1)[0:1]
+
+        def sent(unit, z_first):
+            core_copy(unit).wait_send()
+            for part in range(1 if z_first else 2):
+                y_copy(unit, z_first, part).wait_send()
+            for here in range(4):
+
+                @pl.when(z_at == here)
+                def _(here=here):
+                    for owner in range(4):
+                        if owner > here:
+                            z_copy(unit, owner, 1, z_first, here + 1).wait_send()
+                        if owner < here:
+                            z_copy(unit, owner, -1, z_first, here - 1).wait_send()
+
+            put_copy(unit).wait()
 
         def drain(k, carry):
             @pl.when((k < in_order) & ((k > 1) | second))
@@ -676,82 +738,107 @@
 
             for hop in (1, 2, 3):
 
-                @pl.when((k >= hop) & (k < hop + Z_FIRST[1] - Z_FIRST[0]))
+                @pl.when((k >= LAG[hop]) & (k < LAG[hop] + Z_FIRST))
                 def _(hop=hop):
-                    z_hop(hop, Z_FIRST[0] + k - hop, True)
+                    z_hop(hop, 4 * (k - LAG[hop]), True)
 
             for hop in (1, 2, 3):
 
-                @pl.when((k >= hop) & (k < in_order + hop))
+                @pl.when((k >= LAG[hop]) & (k < in_order + LAG[hop]))
                 def _(hop=hop):
-                    z_hop(hop, unit_at(k - hop), False)
+                    z_hop(hop, unit_at(k - LAG[hop]), False)
 
             for t in range(5):
 
-                @pl.when(k == t + 1)
+                @pl.when(k == SMALL_AT[t])
                 def _(t=t):
                     small_step(t)
 
-            @pl.when((k >= 5) & (k < 5 + Z_FIRST[1] - Z_FIRST[0]))
+            @pl.when((k >= LAG[3] + 1) & (k < LAG[3] + 1 + Z_FIRST))
             def _():
-                finish_z_first(Z_FIRST[0] + k - 5)
+                y_copy(4 * (k - LAG[3] - 1), True).start()
+
+            @pl.when((k >= in_order) & (k < in_order + Z_FIRST))
+            def _():
+                finish_z_first(4 * (k - in_order))
+
+            @pl.when(k == 3)
+            def _():
+                finish_images()
+
+            @pl.when(k >= LAG[3] + 2)
+            def _():
+                sent(unit_at(k - LAG[3] - 2), False)
 
             return carry
 
-        lax.fori_loop(1, in_order + 3, drain, 0)
-
-        def sent(z_first):
-            def body(unit, carry):
-                core_copy(unit).wait_send()
-                y_copy(unit, z_first).wait_send()
-                for here in range(4):
-
-                    @pl.when(z_at == here)
-                    def _(here=here):
-                        for owner in range(4):
-                            if owner > here:
-                                z_copy(unit, owner, 1, z_first, here + 1).wait_send()
-                            if owner < here:
-                                z_copy(unit, owner, -1, z_first, here - 1).wait_send()
-
-                return carry
-
-            return body
-
-        lax.fori_loop(0, Z_FIRST[0], sent(False), 0)
-        lax.fori_loop(*Z_FIRST, sent(True), 0)
-        lax.fori_loop(Z_FIRST[1], UNITS, sent(False), 0)
+        lax.fori_loop(1, in_order + LAG[3], drain, 0)
+
+        for unit in range(0, 4 * Z_FIRST, 4):
+            sent(unit, True)
+        for index in range(in_order - 2, in_order):
+            sent(unit_at(index), False)
         for t in range(5):
             small_send(t).wait_send()
     else:
         r["small"][...] = r["sm"][...] * scale
-        out = pltpu.make_async_copy(wg.at[pl.ds(0, UNITS * width), :], r["grads"], r["pin_sem"])
+        out = pltpu.make_async_copy(wg.at[pl.ds(0, UNITS * width), :], r["grads"], r["pin_sem"].at[0])
         out.start()
         out.wait()
-
-    for img in range(images):
-        bound_copy(img).wait()
-
-        @pl.when(first)
-        def _(img=img):
-            forward_send(img).wait_send()
-
-        @pl.when(second)
-        def _(img=img):
-            backward_send(img).wait_send()
-
-
-def hand_on(count, *refs):
-    given, results, held = refs[:count], refs[count : 2 * count], refs[2 * count : 3 * count]
-    sems = refs[-1]
-    loads = [pltpu.make_async_copy(given[i], held[i], sems.at[0, i]) for i in range(count)]
-    stores = [pltpu.make_async_copy(held[i], results[i], sems.at[1, i]) for i in range(count)]
+        finish_images()
+
+
+def hand_on(bound, grads, small, *refs):
+    out_bound, down, up, out, three = refs[:5]
+    vectors = refs[5:12]
+    held_bound, held_grads, held_small = refs[12:15]
+    held_vectors = refs[15:22]
+    load_sem, store_sem, small_sem, vector_sem = refs[22:]
+    images = bound.shape[0]
+    units, block, width = grads.shape
+
+    def target(unit):
+        if unit < UP:
+            return down.at[:, pl.ds(width * unit, width)]
+        if unit < OUT:
+            return up.at[pl.ds(block * (unit - UP), block), :]
+        if unit < QKV:
+            return out
+        return three.at[pl.ds(block * (unit - QKV), block), :]
+
+    moves = [(bound.at[i], held_bound.at[i], out_bound.at[i]) for i in range(images)]
+    moves += [(grads.at[unit], held_grads.at[unit], target(unit)) for unit in range(units)]
+    loads = [
+        pltpu.make_async_copy(source, held, load_sem.at[i])
+        for i, (source, held, _) in enumerate(moves)
+    ]
+    stores = [
+        pltpu.make_async_copy(held, result, store_sem.at[i])
+        for i, (_, held, result) in enumerate(moves)
+    ]
+    load_small = pltpu.make_async_copy(small, held_small, small_sem)
+    vector_stores = [
+        pltpu.make_async_copy(held, result, vector_sem.at[i])
+        for i, (held, result) in enumerate(zip(held_vectors, vectors))
+    ]
+    load_small.start()
     for load in loads:
         load.start()
+    load_small.wait()
+    gains, shifts, qv, out_vector, up_vector, down_vector, token = held_vectors
+    gains[0] = held_small[0:2, :block]
+    shifts[0] = held_small[2:4, :block]
+    qv[0] = held_small[4:6, :block]
+    out_vector[...] = held_small[6:7, :block]
+    down_vector[...] = held_small[11:12, :block]
+    up_vector[...] = held_small[13:14, : 4 * block]
+    token[...] = held_small[12:13, :].reshape(width)
+    for store in vector_stores:
+        store.start()
     for load, store in zip(loads, stores):
         load.wait()
         store.start()
-    for store in stores:
+    for store in stores + vector_stores:
         store.wait()
 
 
@@ -767,17 +854,12 @@
     block = width // 16
     anywhere = pl.BlockSpec(memory_space=pl.ANY)
     vmem = pl.BlockSpec(memory_space=pltpu.VMEM)
-    shapes = [(images, seq, 1, width)]
+    bound_shape = jax.ShapeDtypeStruct((images, seq, 1, width), F32)
     if reduce_here:
-        shapes += [(block, 4 * width), (4 * block, width), (block, width), (3 * block, width)]
-        shapes += [(1, 2, block)] * 3 + [(1, block), (1, 4 * block), (1, block), (width,)]
-        out_shape = [jax.ShapeDtypeStruct(shape, F32) for shape in shapes]
+        grads_shape = jax.ShapeDtypeStruct((UNITS, block, width), F32)
     else:
-        out_shape = [
-            jax.ShapeDtypeStruct(shapes[0], F32),
-            jax.ShapeDtypeStruct((UNITS * width, width), BF),
-            jax.ShapeDtypeStruct((SMALL, width), F32),
-        ]
+        grads_shape = jax.ShapeDtypeStruct((UNITS * width, width), BF)
+    out_shape = [bound_shape, grads_shape, jax.ShapeDtypeStruct((SMALL, width), F32)]
     narrow = pltpu.VMEM((rows, width), BF)
     dma = pltpu.SemaphoreType.DMA
     scratch = [
@@ -804,7 +886,7 @@
         pltpu.VMEM((SMALL, width), F32),
         pltpu.VMEM((5, SMALL, width), F32),
         pltpu.VMEM((5, SMALL, width), F32),
-        dma(()),
+        dma((images,)),
         dma((UNITS,)),
         dma((images,)),
         dma((images,)),
@@ -813,20 +895,20 @@
         dma((images,)),
     ]
     if reduce_here:
-        z_first = Z_FIRST[1] - Z_FIRST[0]
         scratch += [
+            pltpu.VMEM((UNITS, block, width), F32),
             pltpu.VMEM((UNITS * width // 2, width), BF),
-            pltpu.VMEM((((UNITS - z_first) * 4 + z_first) * block, width), BF),
-            pltpu.VMEM(((UNITS - z_first) * 5 * block, width), BF),
-            pltpu.VMEM((z_first * 10 * block, width), BF),
+            pltpu.VMEM((((UNITS - Z_FIRST) * 4 + Z_FIRST) * block, width), BF),
+            pltpu.VMEM(((UNITS - Z_FIRST) * 5 * block, width), BF),
+            pltpu.VMEM((Z_FIRST * 10 * block, width), BF),
         ]
-        scratch += [dma((UNITS,))] * 4 + [dma((UNITS * 4,))] * 4 + [dma((5,))] * 2
+        scratch += [dma((UNITS,))] * 2 + [dma((UNITS * 2,))] * 2 + [dma((UNITS * 4,))] * 4 + [dma((5,))] * 2 + [dma((UNITS,))]
     weights = 12 * width * width
-    results = pl.pallas_call(
+    bound, grads, small = pl.pallas_call(
         functools.partial(kernel, geo),
         out_shape=out_shape,
         in_specs=[anywhere] * 2 + [vmem] * 8 + [anywhere] * 4,
-        out_specs=[anywhere] + ([vmem] * 11 if reduce_here else [anywhere, vmem]),
+        out_specs=[anywhere, anywhere, vmem],
         scratch_shapes=scratch,
         compiler_params=pltpu.CompilerParams(
             collective_id=0, has_side_effects=True, vmem_limit_bytes=64 * 1024 * 1024 - 65536
@@ -852,20 +934,29 @@
         w_down,
     )
     if reduce_here:
-        count = len(out_shape)
+        shapes = [(block, 4 * width), (4 * block, width), (block, width), (3 * block, width)]
+        shapes += [(1, 2, block)] * 3 + [(1, block), (1, 4 * block), (1, block), (width,)]
         results = pl.pallas_call(
-            functools.partial(hand_on, count),
-            out_shape=out_shape,
-            in_specs=[anywhere] * count,
-            out_specs=[anywhere] * count,
-            scratch_shapes=[pltpu.VMEM(a.shape, a.dtype) for a in out_shape] + [dma((2, count))],
+            hand_on,
+            out_shape=[bound_shape] + [jax.ShapeDtypeStruct(shape, F32) for shape in shapes],
+            in_specs=[anywhere] * 3,
+            out_specs=[anywhere] * 12,
+            scratch_shapes=[
+                pltpu.VMEM(bound_shape.shape, F32),
+                pltpu.VMEM(grads_shape.shape, F32),
+                pltpu.VMEM((SMALL, width), F32),
+                *[pltpu.VMEM(shape, F32) for shape in shapes[4:]],
+                dma((images + UNITS,)),
+                dma((images + UNITS,)),
+                dma(()),
+                dma((len(shapes) - 4,)),
+            ],
             name="hand_on",
-        )(*results)
+        )(bound, grads, small)
         bound, down, up, out, qkv, gains, shifts, qv, out_vector, up_vector, down_vector, token = results
         boundary = bound.transpose(2, 0, 1, 3)
         parts = (boundary, token, gains, shifts, qkv.T[None], qv, out.T[None], out_vector, up.T[None])
-        return (*parts, up_vector, down.reshape(block, 4 * width).T[None], down_vector)
-    bound, grads, small = results
+        return (*parts, up_vector, down.T[None], down_vector)
     me = lax.axis_index("dp")
     share = width // n
     token = lax.psum(small[12], ("dp", "section"))

time: 170 us -> 164 us (0.965)
  Pallas kernels: 169 us -> 163 us
    pallas_call x1, Pallas kernels: 165 us -> 159 us  [on_device(): pl.pallas_call(functools.partial(kernel, geo), out_shape=out_shape, in_sp...]
where the time goes in v4:
time: 164 us
  Pallas kernels  163 us (99%)
    pallas_call x1, Pallas kernels, on_device(): pl.pallas_call(functools.partial(kernel, geo), out_shape=out_shape, in_sp...  159 us
    pallas_call x1, Pallas kernels, on_device(): pl.pallas_call(hand_on, out_shape=[bound_shape] + [jax.ShapeDtypeStruct(s...  4 us

profile of v4, /device:TPU:0, one launch (start us, length us, event | category | flops | bytes accessed | tf_op | source)
XLA Modules:
  0.0 164.1 jit_solution(5506829251325223719)
XLA Ops:
  0.6 159.3 %relay.1 = (f32[3,196,1,768]{3,2,1,0:T(1,128)}, f32[12,48,768]{2,1,0:T(8,128)}, f32[16,768]{1,0:T(8,128)}) custom-call(bf16[3,196,768]{2,1,0:T(8,128)(2,1)} %refs_0_.1, bf16[3,196,768]{2,1,0:T(8,128)(2,1)} %refs_1_.1, s32[3,196]{1,0:T(4,128)} %refs_2_.1, bf16[768]{0:T(1024)(128)(2,1)} %refs_3_.1, f32[2,768]{1,0:T(2,128)} %bitcast.21, f32[2,768]{1,0:T(2,128)} %bitcast.22, ...), custom_call_target="tpu_custom_call" | custom-call | flops 26499612672 | bytes 28311552 | tf_op jit(solution)/shard_map/relay/pallas_call | solution.py:907
  160.0 4.0 %hand_on.1 = (f32[3,196,1,768]{3,2,1,0:T(1,128)}, f32[48,3072]{1,0:T(8,128)}, f32[192,768]{1,0:T(8,128)}, f32[48,768]{1,0:T(8,128)}, f32[144,768]{1,0:T(8,128)},...) custom-call(f32[3,196,1,768]{3,2,1,0:T(1,128)} %get-tuple-element.27, ...), custom_call_target="tpu_custom_call" | custom-call | tf_op jit(solution)/shard_map/hand_on/pallas_call | solution.py:939

commit v5 on v4

--- a/solution.py
+++ b/solution.py
@@ -14,11 +14,11 @@
 F32 = jnp.float32
 Z_FIRST = 2
 WINDOW = 4
-LAG = (0, 1, 2, 3)
+LAG = (0, 1, 3, 5)
 UNITS = 12
 UP, OUT, QKV, DOWN_W = 4, 8, 9, 12
 SMALL = 16
-SMALL_AT = (1, 7, 9, 10, 11)
+SMALL_AT = (1, 7, 10, 12, 13)
 INV_SQRT2 = 1.0 / math.sqrt(2.0)
 INV_SQRT2PI = 1.0 / math.sqrt(2.0 * math.pi)
 

time: 164 us -> 163 us (level)
  no operation moved by 1% of the time
where the time goes in v5:
time: 163 us
  Pallas kernels  162 us (99%)
    pallas_call x1, Pallas kernels, on_device(): pl.pallas_call(functools.partial(kernel, geo), out_shape=out_shape, in_sp...  158 us
    pallas_call x1, Pallas kernels, on_device(): pl.pallas_call(hand_on, out_shape=[bound_shape] + [jax.ShapeDtypeStruct(s...  4 us

profile of v5, /device:TPU:0, one launch (start us, length us, event | category | flops | bytes accessed | tf_op | source)
XLA Modules:
  0.0 162.7 jit_solution(10140235683868209194)
XLA Ops:
  0.6 157.9 %relay.1 = (f32[3,196,1,768]{3,2,1,0:T(1,128)}, f32[12,48,768]{2,1,0:T(8,128)}, f32[16,768]{1,0:T(8,128)}) custom-call(bf16[3,196,768]{2,1,0:T(8,128)(2,1)} %refs_0_.1, bf16[3,196,768]{2,1,0:T(8,128)(2,1)} %refs_1_.1, s32[3,196]{1,0:T(4,128)} %refs_2_.1, bf16[768]{0:T(1024)(128)(2,1)} %refs_3_.1, f32[2,768]{1,0:T(2,128)} %bitcast.21, f32[2,768]{1,0:T(2,128)} %bitcast.22, ...), custom_call_target="tpu_custom_call" | custom-call | flops 26499612672 | bytes 28311552 | tf_op jit(solution)/shard_map/relay/pallas_call | solution.py:907
  158.5 4.0 %hand_on.1 = (f32[3,196,1,768]{3,2,1,0:T(1,128)}, f32[48,3072]{1,0:T(8,128)}, f32[192,768]{1,0:T(8,128)}, f32[48,768]{1,0:T(8,128)}, f32[144,768]{1,0:T(8,128)},...) custom-call(f32[3,196,1,768]{3,2,1,0:T(1,128)} %get-tuple-element.27, ...), custom_call_target="tpu_custom_call" | custom-call | tf_op jit(solution)/shard_map/hand_on/pallas_call | solution.py:939
